TPU v7x, 32 devices: a whole 2x2x4 slice. The times are simulated.
32 devices in a mesh: row: 4 (over x, core), col: 8 (over z, y).
Axes of the slice: x: 2, y: 2, z: 4, core: 2. Of those that a mesh axis runs over, the one named last changes fastest.
Arguments:
- near: float32 [8, 16, 3, 3, 256, 256], P('row', 'col'), may hold values from -0.01 to 3.7
- interp: float32 [8, 16, 160, 160], P('row', 'col'), may hold values from -0.5 to 0.5
- red_count: int32 [8, 16], P('row', 'col'), may hold values from 96 to 160
- owner_flip: int32 [4, 8, 2], P('row', 'col'), may hold values from 0 to 1, as said below
Outputs:
- parents: float32 [4, 8, 640, 640], P('row', 'col')
Inputs may be any that keep to these rules, and one draw needn't show every extreme that they name: owner_flip[i, j, :] is the same on the four devices of each aligned 2 x 2 group, rows 2 i and 2 i + 1, columns 2 j and 2 j + 1.
All inputs are finite; a program needn't handle non-finite values.
Results may differ from a plain program's by a relative error of at most 0.0001.
Values sent between devices are 32-bit elements; how exact they have to be, the bound alone decides.
A program may use at most 128 MiB of HBM per device.

v0:
```python
import jax
import jax.numpy as jnp
from jax import lax
from jax.sharding import PartitionSpec as P

COLOURS = ((0, 0), (0, 1), (1, 0), (1, 1))
STEPS = (-1, 0, 1)
PRECISE = lax.Precision.HIGHEST


def from_partner(value, axis, bit):
    mask = 2**bit
    pairs = [(source, source ^ mask) for source in range(lax.axis_size(axis))]
    return lax.ppermute(value, axis, pairs)


def from_behind(value, axis, by):
    peers = lax.axis_size(axis)
    pairs = [(i, i + by) for i in range(peers) if 0 <= i + by < peers]
    return lax.ppermute(value, axis, pairs)


def owner_rows(parent, flag):
    moved_block = from_partner(parent, "row", 0)
    return jnp.where(flag == 1, moved_block, parent)


def owner_cols(parent, flag):
    moved_block = from_partner(parent, "col", 0)
    return jnp.where(flag == 1, moved_block, parent)


def place_panels(part_panels, row_span, col_span):
    full_panels = jnp.zeros((part_panels.shape[0], 3, 3, part_panels.shape[-1]), jnp.float32)
    return full_panels.at[:, row_span[0] : row_span[1], col_span[0] : col_span[1], :].set(
        part_panels
    )


def apply_updates(store, panels, home_row, home_col, device_row, device_col):
    for row_first in STEPS:
        for col_first in STEPS:
            if (home_row + row_first) // 2 == device_row and (
                home_col + col_first
            ) // 2 == device_col:
                target_row = home_row + row_first - 2 * device_row
                target_col = home_col + col_first - 2 * device_col
                row_low = max(row_first - 1, -1)
                row_high = min(row_first + 1, 1)
                col_low = max(col_first - 1, -1)
                col_high = min(col_first + 1, 1)
                single = panels[:, row_first + 1, col_first + 1, :]
                paired = panels[:, row_low + 1 : row_high + 2, col_low + 1 : col_high + 2, :]
                update = jnp.einsum("rc,rabd->abcd", single, paired, precision=PRECISE)
                store = store.at[
                    target_row,
                    target_col,
                    row_low - row_first + 1 : row_high - row_first + 2,
                    col_low - col_first + 1 : col_high - col_first + 2,
                ].add(-update)
    return store


def local(near, interp, red_count, owner_flip):
    point_count = near.shape[-1]
    slot_count = interp.shape[-1]
    low_start = point_count - slot_count
    slot_index = jnp.arange(slot_count, dtype=jnp.int32)
    point_index = jnp.arange(point_count, dtype=jnp.int32)
    identity = jnp.eye(slot_count, dtype=jnp.float32)
    store = near
    for colour, (home_row, home_col) in enumerate(COLOURS):
        blocks = store[home_row, home_col]
        red_here = red_count[home_row, home_col]
        mask_red = (slot_index < red_here).astype(jnp.float32)
        mask_skel = (slot_index + low_start >= red_here).astype(jnp.float32)
        interp_masked = interp[home_row, home_col] * mask_red[:, None] * mask_skel[None, :]
        reduced = blocks[:, :, :slot_count, :] - jnp.einsum(
            "rs,abst->abrt", interp_masked, blocks[:, :, low_start:, :], precision=PRECISE
        )
        active_rows = []
        for row_step in STEPS:
            line_list = []
            for col_step in STEPS:
                if row_step == 0 and col_step == 0:
                    active_here = point_index >= red_here
                else:
                    active_here = jnp.ones((point_count,), dtype=bool)
                line_list.append(active_here.astype(jnp.float32))
            active_rows.append(jnp.stack(line_list, axis=0))
        active = jnp.stack(active_rows, axis=0)
        inner_rows = reduced * mask_red[None, None, :, None] * active[:, :, None, :]
        centre = reduced[1, 1]
        red_block = centre[:, :slot_count] - jnp.einsum(
            "rt,qt->rq", centre[:, low_start:], interp_masked, precision=PRECISE
        )
        both_masks = mask_red[:, None] * mask_red[None, :]
        padded = jnp.where(both_masks > 0, red_block, identity)
        lower_factor = jnp.linalg.cholesky(padded)
        stacked = inner_rows.transpose(2, 0, 1, 3).reshape(slot_count, 9 * point_count)
        solved = jax.scipy.linalg.solve_triangular(lower_factor, stacked, lower=True)
        panels = solved.reshape(slot_count, 3, 3, point_count)
        step_row = 1 if home_row == 1 else -1
        step_col = 1 if home_col == 1 else -1
        row_span = (1, 3) if step_row == 1 else (0, 2)
        col_span = (1, 3) if step_col == 1 else (0, 2)
        from_side = from_behind(panels[:, :, col_span[0] : col_span[1], :], "col", step_col)
        store = apply_updates(store, panels, home_row, home_col, 0, 0)
        store = apply_updates(
            store, place_panels(from_side, (0, 3), col_span), home_row, home_col, 0, step_col
        )
        from_above, from_corner = from_behind(
            (
                panels[:, row_span[0] : row_span[1], :, :],
                from_side[:, row_span[0] : row_span[1], :, :],
            ),
            "row",
            step_row,
        )
        store = apply_updates(
            store, place_panels(from_above, row_span, (0, 3)), home_row, home_col, step_row, 0
        )
        store = apply_updates(
            store,
            place_panels(from_corner, row_span, col_span),
            home_row,
            home_col,
            step_row,
            step_col,
        )
    mask_child = (slot_index[None, None, :] + low_start >= red_count[:, :, None]).astype(
        jnp.float32
    )
    row_blocks = []
    for first_row, first_col in COLOURS:
        line_list = []
        for second_row, second_col in COLOURS:
            piece_block = store[
                first_row,
                first_col,
                second_row - first_row + 1,
                second_col - first_col + 1,
                low_start:,
                low_start:,
            ]
            piece_block = (
                piece_block
                * mask_child[first_row, first_col][:, None]
                * mask_child[second_row, second_col][None, :]
            )
            line_list.append(piece_block)
        row_blocks.append(jnp.concatenate(line_list, axis=1))
    parent = jnp.concatenate(row_blocks, axis=0)[None, None]
    flip_pair = owner_flip[0, 0]
    parent = owner_rows(parent, flip_pair[0])
    parent = owner_cols(parent, flip_pair[1])
    return parent


def solution(mesh):
    in_specs = (
        P("row", "col", None, None, None, None),
        P("row", "col", None, None),
        P("row", "col"),
        P("row", "col", None),
    )
    out_specs = P("row", "col", None, None)
    return jax.shard_map(local, mesh=mesh, in_specs=in_specs, out_specs=out_specs, check_vma=False)
```

profile of v0, /device:TPU:0, one launch (start us, length us, event | category | flops | bytes accessed | tf_op | source)
XLA Modules:
  0.0 540.1 jit_solution(1995649314608708872)
XLA Ops:
  5.4 9.7 %copy.118 = f32[2,2,3,3,256,256]{4,5,3,2,1,0:T(8,128)} copy(f32[2,2,3,3,256,256]{5,4,3,2,1,0:T(8,128)} %param.103) | data formatting | bytes 18874368 | tf_op args[0]
  21.3 11.7 %cholesky.228 = f32[128,128]{1,0:T(8,128)S(1)} custom-call(f32[128,128]{1,0:T(8,128)S(1)} %cholesky.376), custom_call_target="Cholesky" | custom-call | tf_op jit(solution)/shard_map/jit(cholesky)/cholesky | solution.py:99
  33.0 9.8 %custom-call.17 = f32[1,128,128]{1,2,0:T(8,128)S(1)} custom-call(f32[1,128,128]{2,1,0:T(8,128)S(1)} %get-tuple-element.654), custom_call_target="InvertDiagBlocksLowerTriangular" | custom-call | tf_op jit(solution)/shard_map/jit(cholesky)/cholesky | solution.py:99
  48.9 19.9 %custom-call.18 = f32[2,128,128]{1,2,0:T(8,128)S(1)} custom-call(f32[2,128,128]{2,1,0:T(8,128)S(1)} %pad_maximum_fusion.4), custom_call_target="InvertDiagBlocksLowerTriangular" | custom-call | tf_op jit(solution)/shard_map/jit(_solve_triangular)/triangular_solve | solution.py:101
  79.5 6.9 %fusion.11 = f32[2,2,3,3,256,256]{4,5,3,2,1,0:T(8,128)} fusion(f32[2,2,3,3,256,256]{4,5,3,2,1,0:T(8,128)} %copy.118, f32[160,3,3,256]{3,0,2,1:T(8,128)S(1)} %copy.116), kind=kOutput, calls=%fused_computation.26 | convolution fusion | flops 1133641728 | bytes 6356992 | tf_op jit(solution)/shard_map/rc,rabd->abcd/dot_general | solution.py:54
  140.3 11.7 %cholesky.266 = f32[128,128]{1,0:T(8,128)S(1)} custom-call(f32[128,128]{1,0:T(8,128)S(1)} %cholesky.379), custom_call_target="Cholesky" | custom-call | tf_op jit(solution)/shard_map/jit(cholesky)/cholesky | solution.py:99
  152.1 9.8 %custom-call.19 = f32[1,128,128]{1,2,0:T(8,128)S(1)} custom-call(f32[1,128,128]{2,1,0:T(8,128)S(1)} %get-tuple-element.652), custom_call_target="InvertDiagBlocksLowerTriangular" | custom-call | tf_op jit(solution)/shard_map/jit(cholesky)/cholesky | solution.py:99
  167.8 20.1 %custom-call.20 = f32[2,128,128]{1,2,0:T(8,128)S(1)} custom-call(f32[2,128,128]{2,1,0:T(8,128)S(1)} %pad_maximum_fusion.5), custom_call_target="InvertDiagBlocksLowerTriangular" | custom-call | tf_op jit(solution)/shard_map/jit(_solve_triangular)/triangular_solve | solution.py:101
  199.1 5.6 %collective-permute-start.3 = (f32[160,3,2,256]{3,0,2,1:T(8,128)S(1)}, f32[160,3,2,256]{3,0,2,1:T(8,128)S(1)}, u32[]{:S(2)}, u32[]{:S(2)}) collective-permute-start(f32[160,3,2,256]{3,0,2,1:T(8,128)S(1)} %slice.2697), channel_id=1, source_target_pairs={{0,1},{1,2},{2,3},{3,4},{4,5},{5,6},{6,7},{8,9},{9,10},{10,11},{11... | collective-permute-start | bytes 2949128 | tf_op jit(solution)/shard_map/ppermute | solution.py:20
  206.2 8.4 %fusion.10 = f32[2,2,3,3,256,256]{4,5,3,2,1,0:T(8,128)} fusion(f32[2,2,3,3,256,256]{4,5,3,2,1,0:T(8,128)} %fusion.30, s32[]{:T(128)} %bitcast.86, s32[]{:T(128)} %bitcast.87, f32[160,3,3,256]{3,0,2,1:T(8,128)S(1)} %copy.141), kind=kOutput, calls=%fused_computation.24 | convolution fusion | flops 1133641728 | bytes 6358016 | tf_op jit(solution)/shard_map/rc,rabd->abcd/dot_general | solution.py:54
  218.7 5.3 fusion.29
  241.0 5.3 fusion.27
  257.2 11.7 %cholesky.304 = f32[128,128]{1,0:T(8,128)S(1)} custom-call(f32[128,128]{1,0:T(8,128)S(1)} %cholesky.382), custom_call_target="Cholesky" | custom-call | tf_op jit(solution)/shard_map/jit(cholesky)/cholesky | solution.py:99
  269.0 9.8 %custom-call.21 = f32[1,128,128]{1,2,0:T(8,128)S(1)} custom-call(f32[1,128,128]{2,1,0:T(8,128)S(1)} %get-tuple-element.650), custom_call_target="InvertDiagBlocksLowerTriangular" | custom-call | tf_op jit(solution)/shard_map/jit(cholesky)/cholesky | solution.py:99
  284.8 19.8 %custom-call.22 = f32[2,128,128]{1,2,0:T(8,128)S(1)} custom-call(f32[2,128,128]{2,1,0:T(8,128)S(1)} %pad_maximum_fusion.6), custom_call_target="InvertDiagBlocksLowerTriangular" | custom-call | tf_op jit(solution)/shard_map/jit(_solve_triangular)/triangular_solve | solution.py:101
  325.1 7.1 %fusion.3 = f32[2,2,3,3,256,256]{4,5,3,2,1,0:T(8,128)} fusion(f32[2,2,3,3,256,256]{4,5,3,2,1,0:T(8,128)} %fusion.56, f32[160,3,3,256]{3,0,2,1:T(8,128)S(1)} %copy.166), kind=kOutput, calls=%fused_computation.11 | convolution fusion | flops 1133641728 | bytes 6356992 | tf_op jit(solution)/shard_map/rc,rabd->abcd/dot_general | solution.py:54
  332.2 5.3 fusion.25
  373.4 11.7 %cholesky.342 = f32[128,128]{1,0:T(8,128)S(1)} custom-call(f32[128,128]{1,0:T(8,128)S(1)} %cholesky.385), custom_call_target="Cholesky" | custom-call | tf_op jit(solution)/shard_map/jit(cholesky)/cholesky | solution.py:99
  385.2 9.8 %custom-call.23 = f32[1,128,128]{1,2,0:T(8,128)S(1)} custom-call(f32[1,128,128]{2,1,0:T(8,128)S(1)} %get-tuple-element.648), custom_call_target="InvertDiagBlocksLowerTriangular" | custom-call | tf_op jit(solution)/shard_map/jit(cholesky)/cholesky | solution.py:99
  401.0 19.9 %custom-call.24 = f32[2,128,128]{1,2,0:T(8,128)S(1)} custom-call(f32[2,128,128]{2,1,0:T(8,128)S(1)} %pad_maximum_fusion.7), custom_call_target="InvertDiagBlocksLowerTriangular" | custom-call | tf_op jit(solution)/shard_map/jit(_solve_triangular)/triangular_solve | solution.py:101
  430.9 5.3 collective-permute-start.9
  436.3 5.9 %collective-permute-start.10 = (f32[160,2,3,256]{3,0,2,1:T(8,128)S(1)}, f32[160,2,3,256]{3,0,2,1:T(8,128)S(1)}, u32[]{:S(2)}, u32[]{:S(2)}) collective-permute-start(f32[160,2,3,256]{3,0,2,1:T(8,128)S(1)} %slice.2758), channel_id=1, source_target_pairs={{0,8},{8,16},{16,24},{1,9},{9,17},{17,25},{2,10},{10,18},{18,26},{... | collective-permute-start | bytes 2949128 | tf_op jit(solution)/shard_map/ppermute | solution.py:20
  452.8 7.1 %fusion = f32[2,2,3,3,256,256]{4,5,3,2,1,0:T(8,128)} fusion(f32[2,2,3,3,256,256]{4,5,3,2,1,0:T(8,128)} %fusion.21, f32[160,3,3,256]{3,0,2,1:T(8,128)S(1)} %copy.191), kind=kOutput, calls=%fused_computation.5 | convolution fusion | flops 1133641728 | bytes 6356992 | tf_op jit(solution)/shard_map/rc,rabd->abcd/dot_general | solution.py:54
  502.3 35.7 %collective-permute-done.13 = f32[1,1,640,640]{2,3,1,0:T(8,128)S(1)} collective-permute-done((f32[1,1,640,640]{2,3,1,0:T(8,128)S(1)}, f32[1,1,640,640]{2,3,1,0:T(8,128)S(1)}, u32[]{:S(2)}, u32[]{:S(2)}) %collective-permute-start.13) | collective-permute-done | bytes 1638432 | tf_op jit(solution)/shard_map/ppermute | solution.py:14
  (226 shorter events, 258.8 us)
Async XLA Ops:
  75.5 35.4 %collective-permute-start = (f32[160,3,2,256]{3,0,2,1:T(8,128)}, f32[160,3,2,256]{3,0,2,1:T(8,128)S(1)}, u32[]{:S(2)}, u32[]{:S(2)}) collective-permute-start(f32[160,3,2,256]{3,0,2,1:T(8,128)} %slice.2670), channel_id=1, source_target_pairs={{1,0},{2,1},{3,2},{4,3},{5,4},{6,5},{7,6},{9,8},{10,9},{11,10},{12... | collective-permute-start | bytes 2949128 | tf_op jit(solution)/shard_map/ppermute | solution.py:20
  77.8 44.0 %collective-permute-start.1 = (f32[160,2,3,256]{3,0,2,1:T(8,128)}, f32[160,2,3,256]{3,0,2,1:T(8,128)S(1)}, u32[]{:S(2)}, u32[]{:S(2)}) collective-permute-start(f32[160,2,3,256]{3,0,2,1:T(8,128)} %slice.2675), channel_id=1, source_target_pairs={{8,0},{16,8},{24,16},{9,1},{17,9},{25,17},{10,2},{18,10},{26,18},{... | collective-permute-start | bytes 2949128 | tf_op jit(solution)/shard_map/ppermute | solution.py:20
  88.8 5.9 %copy-start.10 = (s32[2,2]{1,0:T(2,128)S(1)}, s32[2,2]{1,0:T(2,128)}, u32[]{:S(2)}) copy-start(s32[2,2]{1,0:T(2,128)} %param.105) | copy-start | bytes 52
  111.0 20.1 %collective-permute-start.2 = (f32[160,2,2,256]{3,0,2,1:T(8,128)S(1)}, f32[160,2,2,256]{3,0,2,1:T(8,128)S(1)}, u32[]{:S(2)}, u32[]{:S(2)}) collective-permute-start(f32[160,2,2,256]{3,0,2,1:T(8,128)S(1)} %slice.2680), channel_id=1, source_target_pairs={{8,0},{16,8},{24,16},{9,1},{17,9},{25,17},{10,2},{18,10},{26,18},{... | collective-permute-start | bytes 1966088 | tf_op jit(solution)/shard_map/ppermute | solution.py:20
  135.3 1.9 copy-start.2
  135.3 1.9 copy-start.8
  135.3 1.9 copy-start.9
  199.1 26.9 %collective-permute-start.3 = (f32[160,3,2,256]{3,0,2,1:T(8,128)S(1)}, f32[160,3,2,256]{3,0,2,1:T(8,128)S(1)}, u32[]{:S(2)}, u32[]{:S(2)}) collective-permute-start(f32[160,3,2,256]{3,0,2,1:T(8,128)S(1)} %slice.2697), channel_id=1, source_target_pairs={{0,1},{1,2},{2,3},{3,4},{4,5},{5,6},{6,7},{8,9},{9,10},{10,11},{11... | collective-permute-start | bytes 2949128 | tf_op jit(solution)/shard_map/ppermute | solution.py:20
  204.7 32.2 %collective-permute-start.4 = (f32[160,2,3,256]{3,0,2,1:T(8,128)S(1)}, f32[160,2,3,256]{3,0,2,1:T(8,128)S(1)}, u32[]{:S(2)}, u32[]{:S(2)}) collective-permute-start(f32[160,2,3,256]{3,0,2,1:T(8,128)S(1)} %slice.2702), channel_id=1, source_target_pairs={{8,0},{16,8},{24,16},{9,1},{17,9},{25,17},{10,2},{18,10},{26,18},{... | collective-permute-start | bytes 2949128 | tf_op jit(solution)/shard_map/ppermute | solution.py:20
  226.1 20.3 %collective-permute-start.5 = (f32[160,2,2,256]{3,0,2,1:T(8,128)S(1)}, f32[160,2,2,256]{3,0,2,1:T(8,128)S(1)}, u32[]{:S(2)}, u32[]{:S(2)}) collective-permute-start(f32[160,2,2,256]{3,0,2,1:T(8,128)S(1)} %slice.2707), channel_id=1, source_target_pairs={{8,0},{16,8},{24,16},{9,1},{17,9},{25,17},{10,2},{18,10},{26,18},{... | collective-permute-start | bytes 1966088 | tf_op jit(solution)/shard_map/ppermute | solution.py:20
  252.0 1.9 copy-start.6
  252.0 1.9 copy-start.7
  316.0 26.6 %collective-permute-start.6 = (f32[160,3,2,256]{3,0,2,1:T(8,128)S(1)}, f32[160,3,2,256]{3,0,2,1:T(8,128)S(1)}, u32[]{:S(2)}, u32[]{:S(2)}) collective-permute-start(f32[160,3,2,256]{3,0,2,1:T(8,128)S(1)} %slice.2725), channel_id=1, source_target_pairs={{1,0},{2,1},{3,2},{4,3},{5,4},{6,5},{7,6},{9,8},{10,9},{11,10},{12... | collective-permute-start | bytes 2949128 | tf_op jit(solution)/shard_map/ppermute | solution.py:20
  317.3 37.7 %collective-permute-start.7 = (f32[160,2,3,256]{3,0,2,1:T(8,128)S(1)}, f32[160,2,3,256]{3,0,2,1:T(8,128)S(1)}, u32[]{:S(2)}, u32[]{:S(2)}) collective-permute-start(f32[160,2,3,256]{3,0,2,1:T(8,128)S(1)} %slice.2730), channel_id=1, source_target_pairs={{0,8},{8,16},{16,24},{1,9},{9,17},{17,25},{2,10},{10,18},{18,26},{... | collective-permute-start | bytes 2949128 | tf_op jit(solution)/shard_map/ppermute | solution.py:20
  342.6 21.8 %collective-permute-start.8 = (f32[160,2,2,256]{3,0,2,1:T(8,128)S(1)}, f32[160,2,2,256]{3,0,2,1:T(8,128)S(1)}, u32[]{:S(2)}, u32[]{:S(2)}) collective-permute-start(f32[160,2,2,256]{3,0,2,1:T(8,128)S(1)} %slice.2735), channel_id=1, source_target_pairs={{0,8},{8,16},{16,24},{1,9},{9,17},{17,25},{2,10},{10,18},{18,26},{... | collective-permute-start | bytes 1966088 | tf_op jit(solution)/shard_map/ppermute | solution.py:20
  368.4 1.9 copy-start.4
  368.4 1.9 copy-start.5
  430.9 29.0 %collective-permute-start.9 = (f32[160,3,2,256]{3,0,2,1:T(8,128)S(1)}, f32[160,3,2,256]{3,0,2,1:T(8,128)S(1)}, u32[]{:S(2)}, u32[]{:S(2)}) collective-permute-start(f32[160,3,2,256]{3,0,2,1:T(8,128)S(1)} %slice.2753), channel_id=1, source_target_pairs={{0,1},{1,2},{2,3},{3,4},{4,5},{5,6},{6,7},{8,9},{9,10},{10,11},{11... | collective-permute-start | bytes 2949128 | tf_op jit(solution)/shard_map/ppermute | solution.py:20
  436.3 35.4 %collective-permute-start.10 = (f32[160,2,3,256]{3,0,2,1:T(8,128)S(1)}, f32[160,2,3,256]{3,0,2,1:T(8,128)S(1)}, u32[]{:S(2)}, u32[]{:S(2)}) collective-permute-start(f32[160,2,3,256]{3,0,2,1:T(8,128)S(1)} %slice.2758), channel_id=1, source_target_pairs={{0,8},{8,16},{16,24},{1,9},{9,17},{17,25},{2,10},{10,18},{18,26},{... | collective-permute-start | bytes 2949128 | tf_op jit(solution)/shard_map/ppermute | solution.py:20
  460.0 23.7 %collective-permute-start.11 = (f32[160,2,2,256]{3,0,2,1:T(8,128)S(1)}, f32[160,2,2,256]{3,0,2,1:T(8,128)S(1)}, u32[]{:S(2)}, u32[]{:S(2)}) collective-permute-start(f32[160,2,2,256]{3,0,2,1:T(8,128)S(1)} %slice.2761), channel_id=1, source_target_pairs={{0,8},{8,16},{16,24},{1,9},{9,17},{17,25},{2,10},{10,18},{18,26},{... | collective-permute-start | bytes 1966088 | tf_op jit(solution)/shard_map/ppermute | solution.py:20
  477.1 4.2 copy-start.3
  485.8 5.4 %copy-start.11 = (s32[1,1,2]{2,1,0:T(1,128)S(1)}, s32[1,1,2]{2,1,0:T(1,128)}, u32[]{:S(2)}) copy-start(s32[1,1,2]{2,1,0:T(1,128)} %param.106) | copy-start | bytes 28
  490.8 3.6 collective-permute-start.12
  499.1 38.9 %collective-permute-start.13 = (f32[1,1,640,640]{2,3,1,0:T(8,128)S(1)}, f32[1,1,640,640]{2,3,1,0:T(8,128)S(1)}, u32[]{:S(2)}, u32[]{:S(2)}) collective-permute-start(f32[1,1,640,640]{2,3,1,0:T(8,128)S(1)} %broadcast_select_fusion), channel_id=1, source_target_pairs={{0,1},{1,0},{2,3},{3,2},{4,5},{5,4},{6,7},{7,6},{8,9},{9,8},{10,11... | collective-permute-start | bytes 4915208 | tf_op jit(solution)/shard_map/ppermute | solution.py:14
  (2 other events, 3.7 us)
where the time goes:
time: 550 us; the launch traced here: 540 us
  matrix products  207 us (38%)
  other arithmetic  203 us (37%)
  waiting for transfers between devices  44.6 us (8%)
  local copies, waits for them, and re-layouts  39.7 us (7%)
  starting transfers between devices  37.6 us (7%)
  between operations  7.71 us (1%)
    dot_general x36, matrix products, apply_updates(): update = jnp.einsum('rc,rabd->abcd', single, paired, precision=PRECISE)  176 us
    another operation x28, other arithmetic, local(): lower_factor = jnp.linalg.cholesky(padded)  103 us
    another operation x22, other arithmetic, local(): jax.scipy.linalg.solve_triangular(lower_factor, stacked, lower=True)  80.6 us
    ppermute x2, waiting for transfers between devices, from_partner(): return lax.ppermute(value, axis, pairs)  37.6 us
    ppermute x12, starting transfers between devices, from_behind(): return lax.ppermute(value, axis, pairs)  34.6 us
    another operation x12, matrix products, local(): jax.scipy.linalg.solve_triangular(lower_factor, stacked, lower=True)  18.2 us
    unnamed x29, local copies, waits for them, and re-layouts  14.9 us
  transfers between devices with their start and end apart: 14, of which 4 were waited for; matrix products, arithmetic and copies ran while one was open for 30% of the time, Pallas kernels for 0%

commit v1 on v0

v1 whole, which is shorter than its diff:
```python
import functools

import jax
import jax.numpy as jnp
from jax import lax
from jax.experimental import pallas as pl
from jax.experimental.pallas import tpu as pltpu
from jax.sharding import PartitionSpec as P

FULL = (-1, 1, -1, 1)
EXACT = lax.Precision.HIGHEST
GROUP = 8
BLOCK = 32


def split(value):
    high = value.astype(jnp.bfloat16)
    low = (value - high.astype(jnp.float32)).astype(jnp.bfloat16)
    return high, low


def dot(left, right):
    return jnp.dot(left, right, preferred_element_type=jnp.float32)


def product(left, right):
    left_high, left_low = left
    right_high, right_low = right
    return dot(left_high, right_high) + (dot(left_high, right_low) + dot(left_low, right_high))


def left_stack(panel):
    high, low = split(panel.T)
    return high, low


def panel_at(rect, row, col):
    return (row - rect[0]) * (rect[3] - rect[2] + 1) + col - rect[2]


def apply_source(acc, source, rect, target):
    row, col = target
    row_low, row_high = max(row - 1, rect[0]), min(row + 1, rect[1])
    col_low, col_high = max(col - 1, rect[2]), min(col + 1, rect[3])
    width = col_high - col_low + 1
    left = left_stack(source[panel_at(rect, row, col)])

    def body(i, carry):
        row_two = row_low + i // width
        col_two = col_low + i % width
        right = split(source[panel_at(rect, row_two, col_two)])
        at = (row_two - row + 1) * 3 + col_two - col + 1
        acc[at] = acc[at] - product(left, right)
        return carry

    lax.fori_loop(0, (row_high - row_low + 1) * width, body, 0)


def diagonal_inverse(block):
    size = block.shape[0]
    rows = lax.broadcasted_iota(jnp.int32, (size, size), 0)
    cols = lax.broadcasted_iota(jnp.int32, (size, size), 1)
    eye = (rows == cols).astype(jnp.float32)
    wide = jnp.concatenate([block, eye, jnp.zeros((size, 128 - 2 * size), jnp.float32)], axis=1)
    row_ids = lax.broadcasted_iota(jnp.int32, (size, 128), 0)
    scale = jnp.ones((size, 128), jnp.float32)
    for start in range(0, size, GROUP):
        columns = [
            jnp.broadcast_to(wide[:, start + q : start + q + 1], (size, 128)) for q in range(GROUP)
        ]
        for q in range(GROUP):
            at = start + q
            pivot = columns[q][at : at + 1, :]
            inverse = 1.0 / pivot
            below = jnp.where(row_ids > at, columns[q], 0.0)
            scale = jnp.where(row_ids == at, lax.rsqrt(pivot), scale)
            wide = wide - below * (wide[at : at + 1, :] * inverse)
            for p in range(q + 1, GROUP):
                columns[p] = columns[p] - below * (columns[p][at : at + 1, :] * inverse)
    return (wide * scale)[:, size : 2 * size]


def factor_inverse(matrix):
    size = matrix.shape[0]
    rows = lax.broadcasted_iota(jnp.int32, (size, size), 0)
    cols = lax.broadcasted_iota(jnp.int32, (size, size), 1)
    rest = matrix
    right = (rows == cols).astype(jnp.float32)
    done = []
    for start in range(0, size, BLOCK):
        inverse = diagonal_inverse(rest[:BLOCK, :BLOCK])
        top_right = jnp.dot(inverse, right[:BLOCK], precision=EXACT)
        done.append(top_right)
        if start + BLOCK < size:
            top = jnp.dot(inverse, rest[:BLOCK, BLOCK:], precision=EXACT)
            top_t = top.T
            rest = rest[BLOCK:, BLOCK:] - jnp.dot(top_t, top, precision=EXACT)
            right = right[BLOCK:] - jnp.dot(top_t, top_right, precision=EXACT)
    return jnp.concatenate(done, axis=0)


def eliminate_kernel(home, sources, rects_out, keep, *refs):
    n_src, n_out = len(sources), len(rects_out)
    counts, near, interp = refs[:3]
    src = refs[3 : 3 + n_src]
    outs = refs[3 + n_src : 3 + n_src + n_out]
    kept = refs[3 + n_src + n_out] if keep else None
    acc = refs[-1]
    slots = interp.shape[-1]
    points = near.shape[-1]
    low = points - slots
    if n_src:
        for k in range(9):
            acc[k] = near[k]
        for ref, (rect, target) in zip(src, sources):
            apply_source(acc, ref, rect, target)
        store = acc
    else:
        store = near
    if keep:
        for i in range(4):
            a, e = i // 2 - home[0], i % 2 - home[1]
            kept[i] = store[(a + 1) * 3 + e + 1]
    red = counts[home[0], home[1]]
    row_ids = lax.broadcasted_iota(jnp.int32, (slots, slots), 0)
    col_ids = lax.broadcasted_iota(jnp.int32, (slots, slots), 1)
    masked = jnp.where((row_ids < red) & (col_ids + low >= red), interp[...], 0.0)
    centre = store[4]
    reduced = centre[:slots] - jnp.dot(masked, centre[low:], precision=EXACT)
    block = reduced[:, :slots] - lax.dot_general(
        reduced[:, low:], masked, (((1,), (1,)), ((), ())), precision=EXACT
    )
    block = jnp.where(
        (row_ids < red) & (col_ids < red), block, (row_ids == col_ids).astype(jnp.float32)
    )
    block = 0.5 * (block + block.T)
    inverse = split(factor_inverse(block))
    interp_pair = split(masked)
    wide_rows = lax.broadcasted_iota(jnp.int32, (slots, points), 0)
    wide_cols = lax.broadcasted_iota(jnp.int32, (slots, points), 1)
    for k in range(9):
        if k == 4:
            inner = jnp.where((wide_rows < red) & (wide_cols >= red), reduced, 0.0)
        else:
            inner = store[k, :slots] - product(interp_pair, split(store[k, low:]))
            inner = jnp.where(wide_rows < red, inner, 0.0)
        panel = product(inverse, split(inner))
        row, col = k // 3 - 1, k % 3 - 1
        for ref, rect in zip(outs, rects_out):
            if rect[0] <= row <= rect[1] and rect[2] <= col <= rect[3]:
                ref[panel_at(rect, row, col)] = panel


def eliminate(home, counts, near, interp, sources, rects_out, keep):
    points, slots = near.shape[-1], interp.shape[-1]
    rects_out = [FULL] + list(rects_out)
    vmem = pl.BlockSpec(memory_space=pltpu.VMEM)
    out_shape = [
        jax.ShapeDtypeStruct(
            ((r[1] - r[0] + 1) * (r[3] - r[2] + 1), slots, points), jnp.float32
        )
        for r in rects_out
    ]
    if keep:
        out_shape.append(jax.ShapeDtypeStruct((4, points, points), jnp.float32))
    plan = [(rect, target) for _, rect, target in sources]
    return pl.pallas_call(
        functools.partial(eliminate_kernel, home, plan, rects_out, keep),
        out_shape=out_shape,
        in_specs=[pl.BlockSpec(memory_space=pltpu.SMEM)] + [vmem] * (2 + len(sources)),
        out_specs=[vmem] * len(out_shape),
        scratch_shapes=[pltpu.VMEM((9, points, points), jnp.float32)],
        compiler_params=pltpu.CompilerParams(vmem_limit_bytes=56 * 2**20),
        name="eliminate_%d%d" % home,
    )(counts, near, interp, *[array for array, _, _ in sources])


def parent_apply(acc, source, rect, shift, colour):
    boxes = [
        i
        for i in range(4)
        if rect[0] <= i // 2 - shift[0] <= rect[1] and rect[2] <= i % 2 - shift[1] <= rect[3]
    ]
    cols = sorted({i % 2 for i in boxes})
    for x in boxes:
        if x > colour:
            continue
        left = left_stack(source[panel_at(rect, x // 2 - shift[0], x % 2 - shift[1])])

        def body(i, carry, x=x, left=left):
            row = boxes[0] // 2 + i // len(cols)
            col = cols[0] + i % len(cols)
            right = split(source[panel_at(rect, row - shift[0], col - shift[1])])
            at = x * 4 + row * 2 + col
            acc[at] = acc[at] - product(left, right)
            return carry

        lax.fori_loop(0, len(boxes), body, 0)


def parent_first_kernel(plan, near, kept_one, kept_two, kept_three, *refs):
    src, out = refs[:-1], refs[-1]
    for i in range(4):
        out[i] = near[(i // 2 + 1) * 3 + i % 2 + 1]
        out[4 + i] = kept_one[i]
        out[8 + i] = kept_two[i]
        out[12 + i] = kept_three[i]
    for ref, (rect, shift, colour) in zip(src, plan):
        parent_apply(out, ref, rect, shift, colour)


def parent_last_kernel(plan, slots, counts, first, *refs):
    src, out, acc = refs[:-2], refs[-2], refs[-1]
    points = first.shape[-1]
    low = points - slots
    for i in range(16):
        acc[i] = first[i]
    for ref, (rect, shift, colour) in zip(src, plan):
        parent_apply(acc, ref, rect, shift, colour)
    row_ids = lax.broadcasted_iota(jnp.int32, (points, points), 0)
    col_ids = lax.broadcasted_iota(jnp.int32, (points, points), 1)
    for x in range(4):
        for y in range(4):
            keep = (row_ids >= counts[x // 2, x % 2]) & (col_ids >= counts[y // 2, y % 2])
            value = jnp.where(keep, acc[x * 4 + y], 0.0)
            out[x * slots : (x + 1) * slots, y * slots : (y + 1) * slots] = value[low:, low:]


def send(value, axis, by):
    peers = lax.axis_size(axis)
    pairs = [(i, i + by) for i in range(peers) if 0 <= i + by < peers]
    return lax.ppermute(value, axis, pairs)


def from_partner(value, axis):
    pairs = [(source, source ^ 1) for source in range(lax.axis_size(axis))]
    return lax.ppermute(value, axis, pairs)


def local(near, interp, red_count, owner_flip):
    points, slots = near.shape[-1], interp.shape[-1]
    boxes = near.reshape(4, 9, points, points)
    vmem = pl.BlockSpec(memory_space=pltpu.VMEM)
    smem = pl.BlockSpec(memory_space=pltpu.SMEM)

    left0, up0 = (-1, 1, -1, 0), (-1, 0, -1, 1)
    diag0 = (-1, 0, -1, 0)
    w0, l0, u0 = eliminate((0, 0), red_count, boxes[0], interp[0, 0], [], [left0, up0], False)
    l0 = send(l0, "col", -1)
    w1, r1, u1, kept1 = eliminate(
        (0, 1), red_count, boxes[1], interp[0, 1],
        [(w0, FULL, (0, 1)), (l0, left0, (0, -1))],
        [(0, 1, 0, 1), (-1, 0, -1, 1)], True,
    )
    right1, up1, diag1 = (0, 1, 0, 1), (-1, 0, -1, 1), (-1, 0, 0, 1)
    u0 = send(u0, "row", -1)
    d0 = send(l0[0:4], "row", -1)
    r1_mine = send(r1, "col", 1)
    u1 = send(u1, "row", -1)
    d1 = send(u1.reshape(2, 3, slots, points)[:, 1:].reshape(4, slots, points), "col", 1)
    w2, l2, v2, kept2 = eliminate(
        (1, 0), red_count, boxes[2], interp[1, 0],
        [
            (w0, FULL, (1, 0)), (u0, up0, (-1, 0)), (w1, FULL, (1, -1)),
            (r1_mine, right1, (1, 1)), (u1, up1, (-1, -1)), (d1, diag1, (-1, 1)),
        ],
        [(-1, 1, -1, 0), (1, 1, 0, 1)], True,
    )
    left2, down2 = (-1, 1, -1, 0), (1, 1, 0, 1)
    l2 = send(l2, "col", -1)
    v2 = send(v2, "row", 1)
    d2 = send(l2[4:5], "row", 1)
    w3, v3, r3, kept3 = eliminate(
        (1, 1), red_count, boxes[3], interp[1, 1],
        [
            (w0, FULL, (1, 1)), (l0, left0, (1, -1)), (u0, up0, (-1, 1)), (d0, diag0, (-1, -1)),
            (w1, FULL, (1, 0)), (u1, up1, (-1, 0)),
            (w2, FULL, (0, 1)), (l2, left2, (0, -1)),
        ],
        [(1, 1, -1, 0), (-1, 1, 1, 1)], True,
    )
    down3, right3 = (1, 1, -1, 0), (-1, 1, 1, 1)
    v3 = send(v3, "row", 1)
    r3 = send(r3, "col", 1)
    d3 = send(r3[2:3], "row", 1)

    plan_first = [
        (w0, FULL, (0, 0), 0), (w1, FULL, (0, 1), 1), (r1_mine, right1, (0, -1), 1),
        (w2, FULL, (1, 0), 2), (v2, down2, (-1, 0), 2), (l2, left2, (1, 2), 2),
        (d2, (1, 1, -1, -1), (-1, 2), 2), (w3, FULL, (1, 1), 3),
    ]
    first = pl.pallas_call(
        functools.partial(parent_first_kernel, [entry[1:] for entry in plan_first]),
        out_shape=jax.ShapeDtypeStruct((16, points, points), jnp.float32),
        in_specs=[vmem] * (4 + len(plan_first)),
        out_specs=vmem,
        compiler_params=pltpu.CompilerParams(vmem_limit_bytes=56 * 2**20),
        cost_estimate=pl.CostEstimate(
            flops=10 * 10**9, bytes_accessed=20 * 10**6, transcendentals=0
        ),
        name="parent_first",
    )(boxes[0], kept1, kept2, kept3, *[entry[0] for entry in plan_first])
    plan_last = [
        (v3, down3, (-1, 1), 3), (r3, right3, (1, -1), 3), (d3, (1, 1, 1, 1), (-1, -1), 3),
    ]
    parent = pl.pallas_call(
        functools.partial(parent_last_kernel, [entry[1:] for entry in plan_last], slots),
        out_shape=jax.ShapeDtypeStruct((4 * slots, 4 * slots), jnp.float32),
        in_specs=[smem] + [vmem] * (1 + len(plan_last)),
        out_specs=vmem,
        scratch_shapes=[pltpu.VMEM((16, points, points), jnp.float32)],
        compiler_params=pltpu.CompilerParams(vmem_limit_bytes=56 * 2**20),
        name="parent_last",
    )(red_count, first, *[entry[0] for entry in plan_last])
    flip = owner_flip[0, 0]
    parent = jnp.where(flip[0] == 1, from_partner(parent, "row"), parent)
    parent = jnp.where(flip[1] == 1, from_partner(parent, "col"), parent)
    return parent[None, None]


def solution(mesh):
    in_specs = (
        P("row", "col", None, None, None, None),
        P("row", "col", None, None),
        P("row", "col"),
        P("row", "col", None),
    )
    out_specs = P("row", "col", None, None)
    return jax.shard_map(local, mesh=mesh, in_specs=in_specs, out_specs=out_specs, check_vma=False)
```

time: 550 us -> 272 us (0.49); the launches traced: 540 us -> 272 us
  matrix products: 207 us -> 0 us
  other arithmetic: 203 us -> 2.98 us
  Pallas kernels: 0 us -> 106 us
  waiting for transfers between devices: 44.6 us -> 116 us
  local copies, waits for them, and re-layouts: 39.7 us -> 15.1 us
  starting transfers between devices: 37.6 us -> 30.7 us
  between operations: 7.71 us -> 1.52 us
    dot_general x44 -> x0, matrix products: 188 us -> none  [the longest x36 176 us: apply_updates(): update = jnp.einsum('rc,rabd->abcd', single, paired, precision=PRECISE)]
    another operation x52 -> x0, other arithmetic: 184 us -> none  [the longest x28 103 us: local(): lower_factor = jnp.linalg.cholesky(padded)]
    pallas_call x0 -> x6, Pallas kernels: none -> 106 us  [the longest x4 77 us: eliminate(): pl.pallas_call(functools.partial(eliminate_kernel, home, plan, rects_out,...]
    ppermute x12, waiting for transfers between devices: 7.01 us -> 77.7 us  [send(): return lax.ppermute(value, axis, pairs)]
    another operation x20 -> x0, matrix products: 19.5 us -> none  [the longest x12 18.2 us: local(): jax.scipy.linalg.solve_triangular(lower_factor, stacked, lower=True)]
    unnamed x29 -> x34, local copies, waits for them, and re-layouts: 14.9 us -> 4.9 us
    ppermute x12, starting transfers between devices: 34.6 us -> 27.5 us  [send(): return lax.ppermute(value, axis, pairs)]
    convert_element_type x7 -> x0, other arithmetic: 6.76 us -> none  [the longest x4 4.22 us: local(): mask_skel = (slot_index + low_start >= red_here).astype(jnp.float32)]
  transfers between devices with their start and end apart: 14 -> 14, of which waited for: 4 -> 8; matrix products, arithmetic and copies ran while one was open for 30% -> 1% of each run, Pallas kernels for 0% -> 8%
where the time goes in v1:
time: 272 us
  waiting for transfers between devices  116 us (43%)
  Pallas kernels  106 us (39%)
  starting transfers between devices  30.7 us (11%)
  local copies, waits for them, and re-layouts  15.1 us (6%)
  other arithmetic  2.98 us (1%)
    ppermute x12, waiting for transfers between devices, send(): return lax.ppermute(value, axis, pairs)  77.7 us
    pallas_call x4, Pallas kernels, eliminate(): pl.pallas_call(functools.partial(eliminate_kernel, home, plan, rects_out,...  77 us
    ppermute x2, waiting for transfers between devices, from_partner(): return lax.ppermute(value, axis, pairs)  37.8 us
    ppermute x12, starting transfers between devices, send(): return lax.ppermute(value, axis, pairs)  27.5 us
    pallas_call x1, Pallas kernels, local(): pl.pallas_call(functools.partial(parent_first_kernel, [entry[1:] for entr...  21.8 us
    squeeze x1, local copies, waits for them, and re-layouts, local(): boxes[3]  7.61 us
    pallas_call x1, Pallas kernels, local(): pl.pallas_call(functools.partial(parent_last_kernel, [entry[1:] for entry...  7.12 us
  transfers between devices with their start and end apart: 14, of which 8 were waited for; matrix products, arithmetic and copies ran while one was open for 1% of the time, Pallas kernels for 8%

profile of v1, /device:TPU:0, one launch (start us, length us, event | category | flops | bytes accessed | tf_op | source)
XLA Modules:
  0.0 271.8 jit_solution(2132964090168874388)
XLA Ops:
  0.0 7.6 %slice_bitcast_fusion = (f32[9,256,256]{2,1,0:T(8,128)}, f32[9,256,256]{2,1,0:T(8,128)}, f32[9,256,256]{2,1,0:T(8,128)}, f32[9,256,256]{2,1,0:T(8,128)}) fusion(f32[4,9,256,256]{3,2,1,0:T(8,128)} %bitcast.23), kind=kLoop, calls=%fused_computation | loop fusion | bytes 18874368 | tf_op jit(solution)/shard_map/squeeze | solution.py:274
  8.5 11.9 %eliminate_00.1 = (f32[9,160,256]{2,1,0:T(8,128)}, f32[6,160,256]{2,1,0:T(8,128)}, f32[6,160,256]{2,1,0:T(8,128)}) custom-call(s32[2,2]{1,0:T(2,128)} %counts.1, f32[9,256,256]{2,1,0:T(8,128)} %get-tuple-element.38.refs_1_.near, f32[160,160]{1,0:T(8,128)} %get-tuple-element.40.refs_2_), custom_call_target="tpu_custom_call" | custom-call | tf_op jit(solution)/shard_map/eliminate_00/pallas_call | solution.py:167
  21.7 25.6 %collective-permute-done.refs_4_ = f32[6,160,256]{2,1,0:T(8,128)S(1)} collective-permute-done((f32[6,160,256]{2,1,0:T(8,128)}, f32[6,160,256]{2,1,0:T(8,128)S(1)}, u32[]{:S(2)}, u32[]{:S(2)}) %collective-permute-start) | collective-permute-done | bytes 983072 | tf_op jit(solution)/shard_map/ppermute | solution.py:232
  48.2 16.6 %eliminate_01.1 = (f32[9,160,256]{2,1,0:T(8,128)}, f32[4,160,256]{2,1,0:T(8,128)}, f32[6,160,256]{2,1,0:T(8,128)}, f32[4,256,256]{2,1,0:T(8,128)}) custom-call(s32[2,2]{1,0:T(2,128)} %counts.1, f32[9,256,256]{2,1,0:T(8,128)} %get-tuple-element.37.refs_1_, f32[160,160]{1,0:T(8,128)} %get-tuple-element.41.refs_2_, ...), custom_call_target="tpu_custom_call" | custom-call | tf_op jit(solution)/shard_map/eliminate_01/pallas_call | solution.py:167
  67.4 4.6 %collective-permute-start.2 = (f32[4,160,256]{2,1,0:T(8,128)}, f32[4,160,256]{2,1,0:T(8,128)S(1)}, u32[]{:S(2)}, u32[]{:S(2)}) collective-permute-start(f32[4,160,256]{2,1,0:T(8,128)} %get-tuple-element.25), channel_id=1, source_target_pairs={{0,1},{1,2},{2,3},{3,4},{4,5},{5,6},{6,7},{8,9},{9,10},{10,11},{11... | collective-permute-start | bytes 1966088 | tf_op jit(solution)/shard_map/ppermute | solution.py:232
  72.0 2.7 %collective-permute-start.4 = (f32[4,160,256]{2,1,0:T(8,128)S(1)}, f32[4,160,256]{2,1,0:T(8,128)S(1)}, u32[]{:S(2)}, u32[]{:S(2)}) collective-permute-start(f32[4,160,256]{2,1,0:T(8,128)S(1)} %bitcast.25), channel_id=1, source_target_pairs={{0,1},{1,2},{2,3},{3,4},{4,5},{5,6},{6,7},{8,9},{9,10},{10,11},{11... | collective-permute-start | bytes 1966088 | tf_op jit(solution)/shard_map/ppermute | solution.py:232
  74.8 11.8 %collective-permute-done.2.refs_6_.refs_2_ = f32[4,160,256]{2,1,0:T(8,128)S(1)} collective-permute-done((f32[4,160,256]{2,1,0:T(8,128)}, f32[4,160,256]{2,1,0:T(8,128)S(1)}, u32[]{:S(2)}, u32[]{:S(2)}) %collective-permute-start.2) | collective-permute-done | bytes 655392 | tf_op jit(solution)/shard_map/ppermute | solution.py:232
  86.5 13.9 %collective-permute-done.4.refs_8_ = f32[4,160,256]{2,1,0:T(8,128)S(1)} collective-permute-done((f32[4,160,256]{2,1,0:T(8,128)S(1)}, f32[4,160,256]{2,1,0:T(8,128)S(1)}, u32[]{:S(2)}, u32[]{:S(2)}) %collective-permute-start.4) | collective-permute-done | bytes 655392 | tf_op jit(solution)/shard_map/ppermute | solution.py:232
  101.3 22.2 %eliminate_10.1 = (f32[9,160,256]{2,1,0:T(8,128)}, f32[6,160,256]{2,1,0:T(8,128)}, f32[2,160,256]{2,1,0:T(8,128)}, f32[4,256,256]{2,1,0:T(8,128)}) custom-call(s32[2,2]{1,0:T(2,128)} %counts.1, f32[9,256,256]{2,1,0:T(8,128)} %get-tuple-element.36.refs_1_, f32[160,160]{1,0:T(8,128)} %get-tuple-element.42.refs_2_, ...), custom_call_target="tpu_custom_call" | custom-call | tf_op jit(solution)/shard_map/eliminate_10/pallas_call | solution.py:167
  124.9 1.5 collective-permute-start.5
  126.4 2.9 %collective-permute-done.5.refs_6_ = f32[4,160,256]{2,1,0:T(8,128)S(1)} collective-permute-done((f32[4,160,256]{2,1,0:T(8,128)S(1)}, f32[4,160,256]{2,1,0:T(8,128)S(1)}, u32[]{:S(2)}, u32[]{:S(2)}) %collective-permute-start.5) | collective-permute-done | bytes 655392 | tf_op jit(solution)/shard_map/ppermute | solution.py:232
  129.3 21.4 %collective-permute-done.6.refs_10_.refs_5_ = f32[6,160,256]{2,1,0:T(8,128)S(1)} collective-permute-done((f32[6,160,256]{2,1,0:T(8,128)}, f32[6,160,256]{2,1,0:T(8,128)S(1)}, u32[]{:S(2)}, u32[]{:S(2)}) %collective-permute-start.6) | collective-permute-done | bytes 983072 | tf_op jit(solution)/shard_map/ppermute | solution.py:232
  151.6 26.3 %eliminate_11.1 = (f32[9,160,256]{2,1,0:T(8,128)}, f32[2,160,256]{2,1,0:T(8,128)}, f32[3,160,256]{2,1,0:T(8,128)}, f32[4,256,256]{2,1,0:T(8,128)}) custom-call(s32[2,2]{1,0:T(2,128)} %counts.1, f32[9,256,256]{2,1,0:T(8,128)} %get-tuple-element.35.refs_1_, f32[160,160]{1,0:T(8,128)} %get-tuple-element.39.refs_2_, ...), custom_call_target="tpu_custom_call" | custom-call | tf_op jit(solution)/shard_map/eliminate_11/pallas_call | solution.py:167
  178.0 4.5 %collective-permute-start.10 = (f32[3,160,256]{2,1,0:T(8,128)}, f32[3,160,256]{2,1,0:T(8,128)S(1)}, u32[]{:S(2)}, u32[]{:S(2)}) collective-permute-start(f32[3,160,256]{2,1,0:T(8,128)} %get-tuple-element.34), channel_id=1, source_target_pairs={{0,1},{1,2},{2,3},{3,4},{4,5},{5,6},{6,7},{8,9},{9,10},{10,11},{11... | collective-permute-start | bytes 1474568 | tf_op jit(solution)/shard_map/ppermute | solution.py:232
  184.9 4.1 %collective-permute-start.8 = (f32[1,160,256]{2,1,0:T(8,128)S(1)}, f32[1,160,256]{2,1,0:T(8,128)S(1)}, u32[]{:S(2)}, u32[]{:S(2)}) collective-permute-start(f32[1,160,256]{2,1,0:T(8,128)S(1)} %slice.65), channel_id=1, source_target_pairs={{0,8},{8,16},{16,24},{1,9},{9,17},{17,25},{2,10},{10,18},{18,26},{... | collective-permute-start | bytes 491528 | tf_op jit(solution)/shard_map/ppermute | solution.py:232
  189.0 1.9 collective-permute-start.9
  190.9 2.2 collective-permute-done.10.refs_1_
  193.2 1.6 collective-permute-start.11
  195.6 21.8 %parent_first.1.first = f32[16,256,256]{2,1,0:T(8,128)} custom-call(f32[9,256,256]{2,1,0:T(8,128)} %get-tuple-element.38.refs_1_.near, f32[4,256,256]{2,1,0:T(8,128)} %get-tuple-element.22.kept_one, f32[4,256,256]{2,1,0:T(8,128)} %get-tuple-element.27.kept_two, f32[4,256,256]{2,1,0:T(8,128)} %get-tuple-element.30.kept_three, ...), custom_call_target="tpu_custom_call" | custom-call | flops 10000000000 | bytes 20000000 | tf_op jit(solution)/shard_map/parent_first/pallas_call | solution.py:292
  218.8 7.1 %parent_last.1 = f32[640,640]{1,0:T(8,128)} custom-call(s32[2,2]{1,0:T(2,128)} %counts.1, f32[16,256,256]{2,1,0:T(8,128)} %parent_first.1.first, f32[2,160,256]{2,1,0:T(8,128)} %copy-done.10, f32[3,160,256]{2,1,0:T(8,128)} %copy-done.5, f32[1,160,256]{2,1,0:T(8,128)} %copy-done.11), custom_call_target="tpu_custom_call" | custom-call | tf_op jit(solution)/shard_map/parent_last/pallas_call | solution.py:306
  227.9 2.1 collective-permute-done.12
  230.1 1.6 broadcast_select_fusion
  231.7 2.4 collective-permute-start.13
  234.8 35.7 %collective-permute-done.13 = f32[640,640]{1,0:T(8,128)S(1)} collective-permute-done((f32[640,640]{1,0:T(8,128)S(1)}, f32[640,640]{1,0:T(8,128)S(1)}, u32[]{:S(2)}, u32[]{:S(2)}) %collective-permute-start.13) | collective-permute-done | bytes 1638432 | tf_op jit(solution)/shard_map/ppermute | solution.py:237
  (53 shorter events, 16.1 us)
Async XLA Ops:
  0.0 7.6 %copy-start.9 = (f32[2,2,160,160]{3,2,1,0:T(8,128)S(1)}, f32[2,2,160,160]{3,2,1,0:T(8,128)}, u32[]{:S(2)}) copy-start(f32[2,2,160,160]{3,2,1,0:T(8,128)} %param.5) | copy-start | bytes 1228804
  20.4 26.8 %collective-permute-start = (f32[6,160,256]{2,1,0:T(8,128)}, f32[6,160,256]{2,1,0:T(8,128)S(1)}, u32[]{:S(2)}, u32[]{:S(2)}) collective-permute-start(f32[6,160,256]{2,1,0:T(8,128)} %get-tuple-element.21), channel_id=1, source_target_pairs={{1,0},{2,1},{3,2},{4,3},{5,4},{6,5},{7,6},{9,8},{10,9},{11,10},{12... | collective-permute-start | bytes 2949128 | tf_op jit(solution)/shard_map/ppermute | solution.py:232
  48.2 17.9 %copy-start.13 = (f32[6,160,256]{2,1,0:T(8,128)S(1)}, f32[6,160,256]{2,1,0:T(8,128)}, u32[]{:S(2)}) copy-start(f32[6,160,256]{2,1,0:T(8,128)} %get-tuple-element.23) | copy-start | bytes 2949124
  64.8 7.2 %collective-permute-start.3 = (f32[6,160,256]{2,1,0:T(8,128)}, f32[6,160,256]{2,1,0:T(8,128)S(1)}, u32[]{:S(2)}, u32[]{:S(2)}) collective-permute-start(f32[6,160,256]{2,1,0:T(8,128)} %get-tuple-element.26), channel_id=1, source_target_pairs={{8,0},{16,8},{24,16},{9,1},{17,9},{25,17},{10,2},{18,10},{26,18},{... | collective-permute-start | bytes 2949128 | tf_op jit(solution)/shard_map/ppermute | solution.py:232
  66.1 8.7 %collective-permute-start.1 = (f32[6,160,256]{2,1,0:T(8,128)S(1)}, f32[6,160,256]{2,1,0:T(8,128)S(1)}, u32[]{:S(2)}, u32[]{:S(2)}) collective-permute-start(f32[6,160,256]{2,1,0:T(8,128)S(1)} %copy-done.13), channel_id=1, source_target_pairs={{8,0},{16,8},{24,16},{9,1},{17,9},{25,17},{10,2},{18,10},{26,18},{... | collective-permute-start | bytes 2949128 | tf_op jit(solution)/shard_map/ppermute | solution.py:232
  67.4 19.2 %collective-permute-start.2 = (f32[4,160,256]{2,1,0:T(8,128)}, f32[4,160,256]{2,1,0:T(8,128)S(1)}, u32[]{:S(2)}, u32[]{:S(2)}) collective-permute-start(f32[4,160,256]{2,1,0:T(8,128)} %get-tuple-element.25), channel_id=1, source_target_pairs={{0,1},{1,2},{2,3},{3,4},{4,5},{5,6},{6,7},{8,9},{9,10},{10,11},{11... | collective-permute-start | bytes 1966088 | tf_op jit(solution)/shard_map/ppermute | solution.py:232
  71.9 28.5 %copy-start.2 = (f32[6,160,256]{2,1,0:T(8,128)}, f32[6,160,256]{2,1,0:T(8,128)S(1)}, u32[]{:S(2)}) copy-start(f32[6,160,256]{2,1,0:T(8,128)S(1)} %collective-permute-done.3.refs_7_.refs_8_) | copy-start | bytes 2949124
  72.0 28.5 %collective-permute-start.4 = (f32[4,160,256]{2,1,0:T(8,128)S(1)}, f32[4,160,256]{2,1,0:T(8,128)S(1)}, u32[]{:S(2)}, u32[]{:S(2)}) collective-permute-start(f32[4,160,256]{2,1,0:T(8,128)S(1)} %bitcast.25), channel_id=1, source_target_pairs={{0,1},{1,2},{2,3},{3,4},{4,5},{5,6},{6,7},{8,9},{9,10},{10,11},{11... | collective-permute-start | bytes 1966088 | tf_op jit(solution)/shard_map/ppermute | solution.py:232
  74.8 25.7 %copy-start.3 = (f32[6,160,256]{2,1,0:T(8,128)}, f32[6,160,256]{2,1,0:T(8,128)S(1)}, u32[]{:S(2)}) copy-start(f32[6,160,256]{2,1,0:T(8,128)S(1)} %collective-permute-done.1.refs_4_.refs_5_) | copy-start | bytes 2949124
  86.5 13.9 %copy-start.6 = (f32[4,160,256]{2,1,0:T(8,128)}, f32[4,160,256]{2,1,0:T(8,128)S(1)}, u32[]{:S(2)}) copy-start(f32[4,160,256]{2,1,0:T(8,128)S(1)} %collective-permute-done.2.refs_6_.refs_2_) | copy-start | bytes 1966084
  101.3 23.5 %copy-start.1 = (f32[6,160,256]{2,1,0:T(8,128)S(1)}, f32[6,160,256]{2,1,0:T(8,128)}, u32[]{:S(2)}) copy-start(f32[6,160,256]{2,1,0:T(8,128)} %copy-done) | copy-start | bytes 2949124
  123.5 27.1 %collective-permute-start.6 = (f32[6,160,256]{2,1,0:T(8,128)}, f32[6,160,256]{2,1,0:T(8,128)S(1)}, u32[]{:S(2)}, u32[]{:S(2)}) collective-permute-start(f32[6,160,256]{2,1,0:T(8,128)} %get-tuple-element.29), channel_id=1, source_target_pairs={{1,0},{2,1},{3,2},{4,3},{5,4},{6,5},{7,6},{9,8},{10,9},{11,10},{12... | collective-permute-start | bytes 2949128 | tf_op jit(solution)/shard_map/ppermute | solution.py:232
  124.9 4.4 %collective-permute-start.5 = (f32[4,160,256]{2,1,0:T(8,128)S(1)}, f32[4,160,256]{2,1,0:T(8,128)S(1)}, u32[]{:S(2)}, u32[]{:S(2)}) collective-permute-start(f32[4,160,256]{2,1,0:T(8,128)S(1)} %slice.64), channel_id=1, source_target_pairs={{8,0},{16,8},{24,16},{9,1},{17,9},{25,17},{10,2},{18,10},{26,18},{... | collective-permute-start | bytes 1966088 | tf_op jit(solution)/shard_map/ppermute | solution.py:232
  129.3 21.4 %copy-start.7 = (f32[4,160,256]{2,1,0:T(8,128)}, f32[4,160,256]{2,1,0:T(8,128)S(1)}, u32[]{:S(2)}) copy-start(f32[4,160,256]{2,1,0:T(8,128)S(1)} %collective-permute-done.5.refs_6_) | copy-start | bytes 1966084
  151.6 30.9 %copy-start.14 = (f32[2,160,256]{2,1,0:T(8,128)S(1)}, f32[2,160,256]{2,1,0:T(8,128)}, u32[]{:S(2)}) copy-start(f32[2,160,256]{2,1,0:T(8,128)} %get-tuple-element.31) | copy-start | bytes 983044
  178.0 15.2 %collective-permute-start.10 = (f32[3,160,256]{2,1,0:T(8,128)}, f32[3,160,256]{2,1,0:T(8,128)S(1)}, u32[]{:S(2)}, u32[]{:S(2)}) collective-permute-start(f32[3,160,256]{2,1,0:T(8,128)} %get-tuple-element.34), channel_id=1, source_target_pairs={{0,1},{1,2},{2,3},{3,4},{4,5},{5,6},{6,7},{8,9},{9,10},{10,11},{11... | collective-permute-start | bytes 1474568 | tf_op jit(solution)/shard_map/ppermute | solution.py:232
  182.5 12.2 %collective-permute-start.7 = (f32[2,160,256]{2,1,0:T(8,128)S(1)}, f32[2,160,256]{2,1,0:T(8,128)S(1)}, u32[]{:S(2)}, u32[]{:S(2)}) collective-permute-start(f32[2,160,256]{2,1,0:T(8,128)S(1)} %copy-done.14), channel_id=1, source_target_pairs={{0,8},{8,16},{16,24},{1,9},{9,17},{17,25},{2,10},{10,18},{18,26},{... | collective-permute-start | bytes 983048 | tf_op jit(solution)/shard_map/ppermute | solution.py:232
  184.9 9.9 %collective-permute-start.8 = (f32[1,160,256]{2,1,0:T(8,128)S(1)}, f32[1,160,256]{2,1,0:T(8,128)S(1)}, u32[]{:S(2)}, u32[]{:S(2)}) collective-permute-start(f32[1,160,256]{2,1,0:T(8,128)S(1)} %slice.65), channel_id=1, source_target_pairs={{0,8},{8,16},{16,24},{1,9},{9,17},{17,25},{2,10},{10,18},{18,26},{... | collective-permute-start | bytes 491528 | tf_op jit(solution)/shard_map/ppermute | solution.py:232
  189.0 28.4 %collective-permute-start.9 = (f32[2,160,256]{2,1,0:T(8,128)}, f32[2,160,256]{2,1,0:T(8,128)S(1)}, u32[]{:S(2)}, u32[]{:S(2)}) collective-permute-start(f32[2,160,256]{2,1,0:T(8,128)} %get-tuple-element.33), channel_id=1, source_target_pairs={{0,8},{8,16},{16,24},{1,9},{9,17},{17,25},{2,10},{10,18},{18,26},{... | collective-permute-start | bytes 983048 | tf_op jit(solution)/shard_map/ppermute | solution.py:232
  193.2 24.2 %copy-start.5 = (f32[3,160,256]{2,1,0:T(8,128)}, f32[3,160,256]{2,1,0:T(8,128)S(1)}, u32[]{:S(2)}) copy-start(f32[3,160,256]{2,1,0:T(8,128)S(1)} %collective-permute-done.10.refs_1_) | copy-start | bytes 1474564
  193.2 24.2 %collective-permute-start.11 = (f32[1,160,256]{2,1,0:T(8,128)S(1)}, f32[1,160,256]{2,1,0:T(8,128)S(1)}, u32[]{:S(2)}, u32[]{:S(2)}) collective-permute-start(f32[1,160,256]{2,1,0:T(8,128)S(1)} %slice.66), channel_id=1, source_target_pairs={{0,8},{8,16},{16,24},{1,9},{9,17},{17,25},{2,10},{10,18},{18,26},{... | collective-permute-start | bytes 491528 | tf_op jit(solution)/shard_map/ppermute | solution.py:232
  217.4 9.3 %copy-start.12 = (s32[1,1,2]{2,1,0:T(1,128)S(1)}, s32[1,1,2]{2,1,0:T(1,128)}, u32[]{:S(2)}) copy-start(s32[1,1,2]{2,1,0:T(1,128)} %param.7) | copy-start | bytes 28
  225.9 4.1 %collective-permute-start.12 = (f32[640,640]{1,0:T(8,128)}, f32[640,640]{1,0:T(8,128)S(1)}, u32[]{:S(2)}, u32[]{:S(2)}) collective-permute-start(f32[640,640]{1,0:T(8,128)} %parent_last.1), channel_id=1, source_target_pairs={{0,8},{8,0},{16,24},{24,16},{1,9},{9,1},{17,25},{25,17},{2,10},{10... | collective-permute-start | bytes 4915208 | tf_op jit(solution)/shard_map/ppermute | solution.py:237
  231.7 38.8 %collective-permute-start.13 = (f32[640,640]{1,0:T(8,128)S(1)}, f32[640,640]{1,0:T(8,128)S(1)}, u32[]{:S(2)}, u32[]{:S(2)}) collective-permute-start(f32[640,640]{1,0:T(8,128)S(1)} %broadcast_select_fusion), channel_id=1, source_target_pairs={{0,1},{1,0},{2,3},{3,2},{4,5},{5,4},{6,7},{7,6},{8,9},{9,8},{10,11... | collective-permute-start | bytes 4915208 | tf_op jit(solution)/shard_map/ppermute | solution.py:237
  (7 other events, 5.6 us)

commit v2 on v1

--- a/solution.py
+++ b/solution.py
@@ -99,28 +99,34 @@
     return jnp.concatenate(done, axis=0)
 
 
-def eliminate_kernel(home, sources, rects_out, keep, *refs):
+def load(source, at, buffer, sem):
+    view = source if at is None else source.at[at]
+    copy = pltpu.make_async_copy(view, buffer, sem)
+    copy.start()
+    return copy
+
+
+def eliminate_kernel(home, base_at, sources, rects_out, keep, n_extra, *refs):
     n_src, n_out = len(sources), len(rects_out)
-    counts, near, interp = refs[:3]
+    counts, base, interp_all = refs[:3]
     src = refs[3 : 3 + n_src]
-    outs = refs[3 + n_src : 3 + n_src + n_out]
-    kept = refs[3 + n_src + n_out] if keep else None
-    acc = refs[-1]
+    refs = refs[3 + n_src + n_extra :]
+    outs = refs[:n_out]
+    kept = refs[n_out] if keep else None
+    store, interp, sems = refs[-3:]
     slots = interp.shape[-1]
-    points = near.shape[-1]
+    points = store.shape[-1]
     low = points - slots
-    if n_src:
-        for k in range(9):
-            acc[k] = near[k]
-        for ref, (rect, target) in zip(src, sources):
-            apply_source(acc, ref, rect, target)
-        store = acc
-    else:
-        store = near
+    first = load(base, base_at, store, sems.at[0])
+    second = load(interp_all, (home[0], home[1]), interp, sems.at[1])
+    first.wait()
+    second.wait()
+    for ref, (rect, target) in zip(src, sources):
+        apply_source(store, ref, rect, target)
     if keep:
         for i in range(4):
             a, e = i // 2 - home[0], i % 2 - home[1]
-            kept[i] = store[(a + 1) * 3 + e + 1]
+            kept[i] = store[(a + 1) * 3 + e + 1][low:, low:]
     red = counts[home[0], home[1]]
     row_ids = lax.broadcasted_iota(jnp.int32, (slots, slots), 0)
     col_ids = lax.broadcasted_iota(jnp.int32, (slots, slots), 1)
@@ -151,10 +157,21 @@
                 ref[panel_at(rect, row, col)] = panel
 
 
-def eliminate(home, counts, near, interp, sources, rects_out, keep):
-    points, slots = near.shape[-1], interp.shape[-1]
+VMEM = pl.BlockSpec(memory_space=pltpu.VMEM)
+SMEM = pl.BlockSpec(memory_space=pltpu.SMEM)
+ANY = pl.BlockSpec(memory_space=pl.ANY)
+PARAMS = pltpu.CompilerParams(vmem_limit_bytes=56 * 2**20)
+
+
+def cost(products):
+    return pl.CostEstimate(
+        flops=products * 60 * 10**6, bytes_accessed=10**7, transcendentals=0
+    )
+
+
+def eliminate(home, counts, base, base_at, interp, sources, rects_out, keep, extra=()):
+    points, slots = base.shape[-1], interp.shape[-1]
     rects_out = [FULL] + list(rects_out)
-    vmem = pl.BlockSpec(memory_space=pltpu.VMEM)
     out_shape = [
         jax.ShapeDtypeStruct(
             ((r[1] - r[0] + 1) * (r[3] - r[2] + 1), slots, points), jnp.float32
@@ -162,17 +179,49 @@
         for r in rects_out
     ]
     if keep:
-        out_shape.append(jax.ShapeDtypeStruct((4, points, points), jnp.float32))
+        out_shape.append(jax.ShapeDtypeStruct((4, slots, slots), jnp.float32))
     plan = [(rect, target) for _, rect, target in sources]
     return pl.pallas_call(
-        functools.partial(eliminate_kernel, home, plan, rects_out, keep),
+        functools.partial(eliminate_kernel, home, base_at, plan, rects_out, keep, len(extra)),
         out_shape=out_shape,
-        in_specs=[pl.BlockSpec(memory_space=pltpu.SMEM)] + [vmem] * (2 + len(sources)),
-        out_specs=[vmem] * len(out_shape),
-        scratch_shapes=[pltpu.VMEM((9, points, points), jnp.float32)],
-        compiler_params=pltpu.CompilerParams(vmem_limit_bytes=56 * 2**20),
+        in_specs=[SMEM, ANY, ANY] + [VMEM] * len(sources) + [ANY] * len(extra),
+        out_specs=[VMEM] * len(out_shape),
+        scratch_shapes=[
+            pltpu.VMEM((9, points, points), jnp.float32),
+            pltpu.VMEM((slots, slots), jnp.float32),
+            pltpu.SemaphoreType.DMA((2,)),
+        ],
+        compiler_params=PARAMS,
+        cost_estimate=cost(60),
         name="eliminate_%d%d" % home,
-    )(counts, near, interp, *[array for array, _, _ in sources])
+    )(counts, base, interp, *[array for array, _, _ in sources], *extra)
+
+
+def update_kernel(jobs, n_base, n_src, *refs):
+    bases, src = refs[:n_base], refs[n_base : n_base + n_src]
+    outs, sems = refs[n_base + n_src : -1], refs[-1]
+    copies = [
+        load(bases[base], at, out, sems.at[i])
+        for i, ((base, at, _), out) in enumerate(zip(jobs, outs))
+    ]
+    for copy, out, (_, _, work) in zip(copies, outs, jobs):
+        copy.wait()
+        for which, rect, target in work:
+            apply_source(out, src[which], rect, target)
+
+
+def update(name, bases, sources, jobs):
+    points = bases[0].shape[-1]
+    return pl.pallas_call(
+        functools.partial(update_kernel, jobs, len(bases), len(sources)),
+        out_shape=[jax.ShapeDtypeStruct((9, points, points), jnp.float32) for _ in jobs],
+        in_specs=[ANY] * len(bases) + [VMEM] * len(sources),
+        out_specs=[VMEM] * len(jobs),
+        scratch_shapes=[pltpu.SemaphoreType.DMA((len(jobs),))],
+        compiler_params=PARAMS,
+        cost_estimate=cost(20),
+        name=name,
+    )(*bases, *sources)
 
 
 def parent_apply(acc, source, rect, shift, colour):
@@ -182,15 +231,18 @@
         if rect[0] <= i // 2 - shift[0] <= rect[1] and rect[2] <= i % 2 - shift[1] <= rect[3]
     ]
     cols = sorted({i % 2 for i in boxes})
+    slots = acc.shape[-1]
+    low = source.shape[-1] - slots
     for x in boxes:
         if x > colour:
             continue
-        left = left_stack(source[panel_at(rect, x // 2 - shift[0], x % 2 - shift[1])])
+        panel = source[panel_at(rect, x // 2 - shift[0], x % 2 - shift[1])]
+        left = split(panel.T[low:])
 
         def body(i, carry, x=x, left=left):
             row = boxes[0] // 2 + i // len(cols)
             col = cols[0] + i % len(cols)
-            right = split(source[panel_at(rect, row - shift[0], col - shift[1])])
+            right = split(source[panel_at(rect, row - shift[0], col - shift[1])][:, low:])
             at = x * 4 + row * 2 + col
             acc[at] = acc[at] - product(left, right)
             return carry
@@ -198,32 +250,48 @@
         lax.fori_loop(0, len(boxes), body, 0)
 
 
-def parent_first_kernel(plan, near, kept_one, kept_two, kept_three, *refs):
-    src, out = refs[:-1], refs[-1]
+def parent_early_kernel(plan, near, kept_one, kept_two, *refs):
+    src, out, buffer, sems = refs[:-3], refs[-3], refs[-2], refs[-1]
+    low = buffer.shape[-1] - out.shape[-1]
+    copies = [
+        load(near, (0, (i // 2 + 1) * 3 + i % 2 + 1), buffer.at[i], sems.at[i]) for i in range(4)
+    ]
     for i in range(4):
-        out[i] = near[(i // 2 + 1) * 3 + i % 2 + 1]
+        copies[i].wait()
+        out[i] = buffer[i][low:, low:]
         out[4 + i] = kept_one[i]
         out[8 + i] = kept_two[i]
+        out[12 + i] = jnp.zeros(out.shape[1:], jnp.float32)
+    for ref, (rect, shift, colour) in zip(src, plan):
+        parent_apply(out, ref, rect, shift, colour)
+
+
+def parent_middle_kernel(plan, early, kept_three, *refs):
+    src, out = refs[:-1], refs[-1]
+    for i in range(12):
+        out[i] = early[i]
+    for i in range(4):
         out[12 + i] = kept_three[i]
     for ref, (rect, shift, colour) in zip(src, plan):
         parent_apply(out, ref, rect, shift, colour)
 
 
-def parent_last_kernel(plan, slots, counts, first, *refs):
+def parent_last_kernel(plan, points, counts, middle, *refs):
     src, out, acc = refs[:-2], refs[-2], refs[-1]
-    points = first.shape[-1]
+    slots = acc.shape[-1]
     low = points - slots
     for i in range(16):
-        acc[i] = first[i]
+        acc[i] = middle[i]
     for ref, (rect, shift, colour) in zip(src, plan):
         parent_apply(acc, ref, rect, shift, colour)
-    row_ids = lax.broadcasted_iota(jnp.int32, (points, points), 0)
-    col_ids = lax.broadcasted_iota(jnp.int32, (points, points), 1)
+    row_ids = lax.broadcasted_iota(jnp.int32, (slots, slots), 0) + low
+    col_ids = lax.broadcasted_iota(jnp.int32, (slots, slots), 1) + low
     for x in range(4):
         for y in range(4):
             keep = (row_ids >= counts[x // 2, x % 2]) & (col_ids >= counts[y // 2, y % 2])
-            value = jnp.where(keep, acc[x * 4 + y], 0.0)
-            out[x * slots : (x + 1) * slots, y * slots : (y + 1) * slots] = value[low:, low:]
+            out[x * slots : (x + 1) * slots, y * slots : (y + 1) * slots] = jnp.where(
+                keep, acc[x * 4 + y], 0.0
+            )
 
 
 def send(value, axis, by):
@@ -240,78 +308,99 @@
 def local(near, interp, red_count, owner_flip):
     points, slots = near.shape[-1], interp.shape[-1]
     boxes = near.reshape(4, 9, points, points)
-    vmem = pl.BlockSpec(memory_space=pltpu.VMEM)
-    smem = pl.BlockSpec(memory_space=pltpu.SMEM)
-
-    left0, up0 = (-1, 1, -1, 0), (-1, 0, -1, 1)
-    diag0 = (-1, 0, -1, 0)
-    w0, l0, u0 = eliminate((0, 0), red_count, boxes[0], interp[0, 0], [], [left0, up0], False)
+
+    left0, up0, diag0 = (-1, 1, -1, 0), (-1, 0, -1, 1), (-1, 0, -1, 0)
+    right1, up1, diag1 = (0, 1, 0, 1), (-1, 0, -1, 1), (-1, 0, 0, 1)
+    left2, down2 = (-1, 1, -1, 0), (1, 1, 0, 1)
+    down3, right3 = (1, 1, -1, 0), (-1, 0, 1, 1)
+    corner3 = (1, 1, 1, 1)
+
+    w0, l0, u0 = eliminate(
+        (0, 0), red_count, boxes, 0, interp, [], [left0, up0], False
+    )
     l0 = send(l0, "col", -1)
+    u0 = send(u0, "row", -1)
+    acc1, acc2, acc3 = update(
+        "gap_zero", [boxes], [w0],
+        [(0, i, [(0, FULL, (i // 2, i % 2))]) for i in (1, 2, 3)],
+    )
     w1, r1, u1, kept1 = eliminate(
-        (0, 1), red_count, boxes[1], interp[0, 1],
-        [(w0, FULL, (0, 1)), (l0, left0, (0, -1))],
-        [(0, 1, 0, 1), (-1, 0, -1, 1)], True,
-    )
-    right1, up1, diag1 = (0, 1, 0, 1), (-1, 0, -1, 1), (-1, 0, 0, 1)
-    u0 = send(u0, "row", -1)
+        (0, 1), red_count, acc1, None, interp, [(l0, left0, (0, -1))], [right1, up1], True,
+        extra=(u0,),
+    )
     d0 = send(l0[0:4], "row", -1)
-    r1_mine = send(r1, "col", 1)
+    r1 = send(r1, "col", 1)
     u1 = send(u1, "row", -1)
     d1 = send(u1.reshape(2, 3, slots, points)[:, 1:].reshape(4, slots, points), "col", 1)
+    acc2, acc3 = update(
+        "gap_one", [acc2, acc3], [u0, w1, l0],
+        [
+            (0, None, [(0, up0, (-1, 0)), (1, FULL, (1, -1))]),
+            (1, None, [(0, up0, (-1, 1)), (1, FULL, (1, 0)), (2, left0, (1, -1))]),
+        ],
+    )
     w2, l2, v2, kept2 = eliminate(
-        (1, 0), red_count, boxes[2], interp[1, 0],
-        [
-            (w0, FULL, (1, 0)), (u0, up0, (-1, 0)), (w1, FULL, (1, -1)),
-            (r1_mine, right1, (1, 1)), (u1, up1, (-1, -1)), (d1, diag1, (-1, 1)),
-        ],
-        [(-1, 1, -1, 0), (1, 1, 0, 1)], True,
-    )
-    left2, down2 = (-1, 1, -1, 0), (1, 1, 0, 1)
+        (1, 0), red_count, acc2, None, interp,
+        [(r1, right1, (1, 1)), (u1, up1, (-1, -1)), (d1, diag1, (-1, 1))],
+        [left2, down2], True, extra=(d0,),
+    )
     l2 = send(l2, "col", -1)
     v2 = send(v2, "row", 1)
-    d2 = send(l2[4:5], "row", 1)
-    w3, v3, r3, kept3 = eliminate(
-        (1, 1), red_count, boxes[3], interp[1, 1],
-        [
-            (w0, FULL, (1, 1)), (l0, left0, (1, -1)), (u0, up0, (-1, 1)), (d0, diag0, (-1, -1)),
-            (w1, FULL, (1, 0)), (u1, up1, (-1, 0)),
-            (w2, FULL, (0, 1)), (l2, left2, (0, -1)),
+    (acc3,) = update(
+        "gap_two", [acc3], [d0, u1, w2],
+        [(0, None, [(0, diag0, (-1, -1)), (1, up1, (-1, 0)), (2, FULL, (0, 1))])],
+    )
+    plan_early = [
+        (w0, FULL, (0, 0), 0), (w1, FULL, (0, 1), 1), (r1, right1, (0, -1), 1),
+        (w2, FULL, (1, 0), 2),
+    ]
+    early = pl.pallas_call(
+        functools.partial(parent_early_kernel, [entry[1:] for entry in plan_early]),
+        out_shape=jax.ShapeDtypeStruct((16, slots, slots), jnp.float32),
+        in_specs=[ANY] + [VMEM] * (2 + len(plan_early)),
+        out_specs=VMEM,
+        scratch_shapes=[
+            pltpu.VMEM((4, points, points), jnp.float32), pltpu.SemaphoreType.DMA((4,)),
         ],
-        [(1, 1, -1, 0), (-1, 1, 1, 1)], True,
-    )
-    down3, right3 = (1, 1, -1, 0), (-1, 1, 1, 1)
+        compiler_params=PARAMS,
+        cost_estimate=cost(30),
+        name="parent_early",
+    )(boxes, kept1, kept2, *[entry[0] for entry in plan_early])
+    w3, v3, r3, d3, kept3 = eliminate(
+        (1, 1), red_count, acc3, None, interp, [(l2, left2, (0, -1))],
+        [down3, right3, corner3], True, extra=(early, v2),
+    )
     v3 = send(v3, "row", 1)
     r3 = send(r3, "col", 1)
-    d3 = send(r3[2:3], "row", 1)
-
-    plan_first = [
-        (w0, FULL, (0, 0), 0), (w1, FULL, (0, 1), 1), (r1_mine, right1, (0, -1), 1),
-        (w2, FULL, (1, 0), 2), (v2, down2, (-1, 0), 2), (l2, left2, (1, 2), 2),
+    d3 = send(send(d3, "row", 1), "col", 1)
+    d2 = send(l2[4:5], "row", 1)
+
+    plan_middle = [
+        (v2, down2, (-1, 0), 2), (l2, left2, (1, 2), 2),
         (d2, (1, 1, -1, -1), (-1, 2), 2), (w3, FULL, (1, 1), 3),
     ]
-    first = pl.pallas_call(
-        functools.partial(parent_first_kernel, [entry[1:] for entry in plan_first]),
-        out_shape=jax.ShapeDtypeStruct((16, points, points), jnp.float32),
-        in_specs=[vmem] * (4 + len(plan_first)),
-        out_specs=vmem,
-        compiler_params=pltpu.CompilerParams(vmem_limit_bytes=56 * 2**20),
-        cost_estimate=pl.CostEstimate(
-            flops=10 * 10**9, bytes_accessed=20 * 10**6, transcendentals=0
-        ),
-        name="parent_first",
-    )(boxes[0], kept1, kept2, kept3, *[entry[0] for entry in plan_first])
+    middle = pl.pallas_call(
+        functools.partial(parent_middle_kernel, [entry[1:] for entry in plan_middle]),
+        out_shape=jax.ShapeDtypeStruct((16, slots, slots), jnp.float32),
+        in_specs=[VMEM] * (2 + len(plan_middle)),
+        out_specs=VMEM,
+        compiler_params=PARAMS,
+        cost_estimate=cost(30),
+        name="parent_middle",
+    )(early, kept3, *[entry[0] for entry in plan_middle])
     plan_last = [
-        (v3, down3, (-1, 1), 3), (r3, right3, (1, -1), 3), (d3, (1, 1, 1, 1), (-1, -1), 3),
+        (v3, down3, (-1, 1), 3), (r3, right3, (1, -1), 3), (d3, corner3, (-1, -1), 3),
     ]
     parent = pl.pallas_call(
-        functools.partial(parent_last_kernel, [entry[1:] for entry in plan_last], slots),
+        functools.partial(parent_last_kernel, [entry[1:] for entry in plan_last], points),
         out_shape=jax.ShapeDtypeStruct((4 * slots, 4 * slots), jnp.float32),
-        in_specs=[smem] + [vmem] * (1 + len(plan_last)),
-        out_specs=vmem,
-        scratch_shapes=[pltpu.VMEM((16, points, points), jnp.float32)],
-        compiler_params=pltpu.CompilerParams(vmem_limit_bytes=56 * 2**20),
+        in_specs=[SMEM] + [VMEM] * (1 + len(plan_last)),
+        out_specs=VMEM,
+        scratch_shapes=[pltpu.VMEM((16, slots, slots), jnp.float32)],
+        compiler_params=PARAMS,
+        cost_estimate=cost(10),
         name="parent_last",
-    )(red_count, first, *[entry[0] for entry in plan_last])
+    )(red_count, middle, *[entry[0] for entry in plan_last])
     flip = owner_flip[0, 0]
     parent = jnp.where(flip[0] == 1, from_partner(parent, "row"), parent)
     parent = jnp.where(flip[1] == 1, from_partner(parent, "col"), parent)

time: 272 us -> 239 us (0.88)
  waiting for transfers between devices: 116 us -> 64.4 us
  Pallas kernels: 106 us -> 126 us
  local copies, waits for them, and re-layouts: 15.1 us -> 8.72 us
  starting transfers between devices: 30.7 us -> 34.1 us
    ppermute x12 -> x13, waiting for transfers between devices: 77.7 us -> 25.2 us  [send(): return lax.ppermute(value, axis, pairs)]
    pallas_call x5 -> x9, Pallas kernels: 98.9 us -> 119 us  [the longest x4 59.2 us: eliminate(): pl.pallas_call(functools.partial(eliminate_kernel, home, base_at, plan, r...]
    squeeze x2 -> x0, local copies, waits for them, and re-layouts: 8.5 us -> none  [the longest x1 7.61 us: local(): boxes[3]]
    ppermute x12 -> x13, starting transfers between devices: 27.5 us -> 33.5 us  [send(): return lax.ppermute(value, axis, pairs)]
    unnamed x34 -> x26, local copies, waits for them, and re-layouts: 4.9 us -> 5.99 us
  transfers between devices with their start and end apart: 14 -> 15, of which waited for: 8 -> 4; matrix products, arithmetic and copies ran while one was open for 1% -> 1% of each run, Pallas kernels for 8% -> 25%
where the time goes in v2:
time: 239 us; the launch traced here: 238 us
  Pallas kernels  126 us (53%)
  waiting for transfers between devices  64.4 us (27%)
  starting transfers between devices  34.1 us (14%)
  local copies, waits for them, and re-layouts  8.72 us (4%)
  other arithmetic  2.98 us (1%)
    pallas_call x4, Pallas kernels, eliminate(): pl.pallas_call(functools.partial(eliminate_kernel, home, base_at, plan, r...  59.2 us
    ppermute x2, waiting for transfers between devices, from_partner(): return lax.ppermute(value, axis, pairs)  39.2 us
    ppermute x13, starting transfers between devices, send(): return lax.ppermute(value, axis, pairs)  33.5 us
    pallas_call x3, Pallas kernels, update(): pl.pallas_call(functools.partial(update_kernel, jobs, len(bases), len(sou...  32.6 us
    ppermute x13, waiting for transfers between devices, send(): return lax.ppermute(value, axis, pairs)  25.2 us
    pallas_call x1, Pallas kernels, local(): pl.pallas_call(functools.partial(parent_early_kernel, [entry[1:] for entr...  14.9 us
    pallas_call x1, Pallas kernels, local(): pl.pallas_call(functools.partial(parent_middle_kernel, [entry[1:] for ent...  12.5 us
    pallas_call x1, Pallas kernels, local(): pl.pallas_call(functools.partial(parent_last_kernel, [entry[1:] for entry...  6.89 us
  transfers between devices with their start and end apart: 15, of which 4 were waited for; matrix products, arithmetic and copies ran while one was open for 1% of the time, Pallas kernels for 25%

profile of v2, /device:TPU:0, one launch (start us, length us, event | category | flops | bytes accessed | tf_op | source)
XLA Modules:
  0.0 237.8 jit_solution(5684966490583734296)
XLA Ops:
  0.0 12.6 %eliminate_00.1 = (f32[9,160,256]{2,1,0:T(8,128)}, f32[6,160,256]{2,1,0:T(8,128)}, f32[6,160,256]{2,1,0:T(8,128)}) custom-call(s32[2,2]{1,0:T(2,128)} %counts.1, f32[4,9,256,256]{3,2,1,0:T(8,128)} %bitcast.7, f32[2,2,160,160]{3,2,1,0:T(8,128)} %refs_2_.7), custom_call_target="tpu_custom_call" | custom-call | flops 3600000000 | bytes 10000000 | tf_op jit(solution)/shard_map/eliminate_00/pallas_call | solution.py:184
  15.2 10.3 %gap_zero.1 = (f32[9,256,256]{2,1,0:T(8,128)}, f32[9,256,256]{2,1,0:T(8,128)}, f32[9,256,256]{2,1,0:T(8,128)}) custom-call(f32[4,9,256,256]{3,2,1,0:T(8,128)} %bitcast.8, f32[9,160,256]{2,1,0:T(8,128)} %get-tuple-element.26.refs_1_.refs_0_), custom_call_target="tpu_custom_call" | custom-call | flops 1200000000 | bytes 10000000 | tf_op jit(solution)/shard_map/gap_zero/pallas_call | solution.py:215
  25.5 13.9 %collective-permute-done.refs_3_.refs_4_ = f32[6,160,256]{2,1,0:T(8,128)S(1)} collective-permute-done((f32[6,160,256]{2,1,0:T(8,128)}, f32[6,160,256]{2,1,0:T(8,128)S(1)}, u32[]{:S(2)}, u32[]{:S(2)}) %collective-permute-start) | collective-permute-done | bytes 983072 | tf_op jit(solution)/shard_map/ppermute | solution.py:300
  40.8 14.9 %eliminate_01.1 = (f32[9,160,256]{2,1,0:T(8,128)}, f32[4,160,256]{2,1,0:T(8,128)}, f32[6,160,256]{2,1,0:T(8,128)}, f32[4,160,160]{2,1,0:T(8,128)}) custom-call(s32[2,2]{1,0:T(2,128)} %counts.1, f32[9,256,256]{2,1,0:T(8,128)} %get-tuple-element.27.refs_1_, f32[2,2,160,160]{3,2,1,0:T(8,128)} %refs_2_.7, f32[6,160,256]{2,1,0:T(8,128)} %copy-done.1, ...), custom_call_target="tpu_custom_call" | custom-call | flops 3600000000 | bytes 10000000 | tf_op jit(solution)/shard_map/eliminate_01/pallas_call | solution.py:184
  57.0 4.6 %collective-permute-start.2 = (f32[4,160,256]{2,1,0:T(8,128)}, f32[4,160,256]{2,1,0:T(8,128)S(1)}, u32[]{:S(2)}, u32[]{:S(2)}) collective-permute-start(f32[4,160,256]{2,1,0:T(8,128)} %get-tuple-element.35), channel_id=1, source_target_pairs={{0,1},{1,2},{2,3},{3,4},{4,5},{5,6},{6,7},{8,9},{9,10},{10,11},{11... | collective-permute-start | bytes 1966088 | tf_op jit(solution)/shard_map/ppermute | solution.py:300
  64.1 2.7 %collective-permute-start.4 = (f32[4,160,256]{2,1,0:T(8,128)S(1)}, f32[4,160,256]{2,1,0:T(8,128)S(1)}, u32[]{:S(2)}, u32[]{:S(2)}) collective-permute-start(f32[4,160,256]{2,1,0:T(8,128)S(1)} %bitcast.11), channel_id=1, source_target_pairs={{0,1},{1,2},{2,3},{3,4},{4,5},{5,6},{6,7},{8,9},{9,10},{10,11},{11... | collective-permute-start | bytes 1966088 | tf_op jit(solution)/shard_map/ppermute | solution.py:300
  66.8 12.6 %gap_one.1 = (f32[9,256,256]{2,1,0:T(8,128)}, f32[9,256,256]{2,1,0:T(8,128)}) custom-call(f32[9,256,256]{2,1,0:T(8,128)} %get-tuple-element.31.refs_0_, f32[9,256,256]{2,1,0:T(8,128)} %get-tuple-element.32.refs_1_, f32[6,160,256]{2,1,0:T(8,128)} %copy-done.3, f32[9,160,256]{2,1,0:T(8,128)} %get-tuple-element.33.refs_3_.refs_1_, f32[6,160,256]{2,1,0:T(8,128)} %copy-done.1), custom_call_target="tpu_custom_call" | custom-call | flops 1200000000 | bytes 10000000 | tf_op jit(solution)/shard_map/gap_one/pallas_call | solution.py:215
  79.4 11.3 %collective-permute-done.4.refs_5_ = f32[4,160,256]{2,1,0:T(8,128)S(1)} collective-permute-done((f32[4,160,256]{2,1,0:T(8,128)S(1)}, f32[4,160,256]{2,1,0:T(8,128)S(1)}, u32[]{:S(2)}, u32[]{:S(2)}) %collective-permute-start.4) | collective-permute-done | bytes 655392 | tf_op jit(solution)/shard_map/ppermute | solution.py:300
  91.6 17.1 %eliminate_10.1 = (f32[9,160,256]{2,1,0:T(8,128)}, f32[6,160,256]{2,1,0:T(8,128)}, f32[2,160,256]{2,1,0:T(8,128)}, f32[4,160,160]{2,1,0:T(8,128)}) custom-call(s32[2,2]{1,0:T(2,128)} %counts.1, f32[9,256,256]{2,1,0:T(8,128)} %get-tuple-element.34.refs_1_, f32[2,2,160,160]{3,2,1,0:T(8,128)} %refs_2_.7, f32[4,160,256]{2,1,0:T(8,128)} %copy-done.4, ...), custom_call_target="tpu_custom_call" | custom-call | flops 3600000000 | bytes 10000000 | tf_op jit(solution)/shard_map/eliminate_10/pallas_call | solution.py:184
  110.0 2.5 %collective-permute-start.7 = (f32[2,160,256]{2,1,0:T(8,128)}, f32[2,160,256]{2,1,0:T(8,128)S(1)}, u32[]{:S(2)}, u32[]{:S(2)}) collective-permute-start(f32[2,160,256]{2,1,0:T(8,128)} %get-tuple-element.41), channel_id=1, source_target_pairs={{0,8},{8,16},{16,24},{1,9},{9,17},{17,25},{2,10},{10,18},{18,26},{... | collective-permute-start | bytes 983048 | tf_op jit(solution)/shard_map/ppermute | solution.py:300
  112.5 9.7 %gap_two.1.refs_1_ = f32[9,256,256]{2,1,0:T(8,128)} custom-call(f32[9,256,256]{2,1,0:T(8,128)} %get-tuple-element.39.refs_0_, f32[4,160,256]{2,1,0:T(8,128)} %copy-done.5, f32[6,160,256]{2,1,0:T(8,128)} %copy-done, f32[9,160,256]{2,1,0:T(8,128)} %get-tuple-element.38.refs_3_), custom_call_target="tpu_custom_call" | custom-call | flops 1200000000 | bytes 10000000 | tf_op jit(solution)/shard_map/gap_two/pallas_call | solution.py:215
  122.1 14.9 %parent_early.1.refs_4_.early = f32[16,160,160]{2,1,0:T(8,128)} custom-call(f32[4,9,256,256]{3,2,1,0:T(8,128)} %bitcast.9, f32[4,160,160]{2,1,0:T(8,128)} %get-tuple-element.30.kept_one, f32[4,160,160]{2,1,0:T(8,128)} %get-tuple-element.37.kept_two, f32[9,160,256]{2,1,0:T(8,128)} %get-tuple-element.26.refs_1_.refs_0_, ...), custom_call_target="tpu_custom_call" | custom-call | flops 1800000000 | bytes 10000000 | tf_op jit(solution)/shard_map/parent_early/pallas_call | solution.py:357
  138.7 14.7 %eliminate_11.1 = (f32[9,160,256]{2,1,0:T(8,128)}, f32[2,160,256]{2,1,0:T(8,128)}, f32[2,160,256]{2,1,0:T(8,128)}, f32[1,160,256]{2,1,0:T(8,128)}, f32[4,160,160]{2,1,0:T(8,128)}) custom-call(s32[2,2]{1,0:T(2,128)} %counts.1, f32[9,256,256]{2,1,0:T(8,128)} %gap_two.1.refs_1_, f32[2,2,160,160]{3,2,1,0:T(8,128)} %refs_2_.7, f32[6,160,256]{2,1,0:T(8,128)} %copy-done.2, ...), custom_call_target="tpu_custom_call" | custom-call | flops 3600000000 | bytes 10000000 | tf_op jit(solution)/shard_map/eliminate_11/pallas_call | solution.py:184
  153.4 3.5 %collective-permute-start.11 = (f32[1,160,256]{2,1,0:T(8,128)}, f32[1,160,256]{2,1,0:T(8,128)S(1)}, u32[]{:S(2)}, u32[]{:S(2)}) collective-permute-start(f32[1,160,256]{2,1,0:T(8,128)} %get-tuple-element.46), channel_id=1, source_target_pairs={{0,8},{8,16},{16,24},{1,9},{9,17},{17,25},{2,10},{10,18},{18,26},{... | collective-permute-start | bytes 491528 | tf_op jit(solution)/shard_map/ppermute | solution.py:300
  157.8 1.9 collective-permute-start.8
  159.8 5.0 %collective-permute-start.10 = (f32[2,160,256]{2,1,0:T(8,128)}, f32[2,160,256]{2,1,0:T(8,128)S(1)}, u32[]{:S(2)}, u32[]{:S(2)}) collective-permute-start(f32[2,160,256]{2,1,0:T(8,128)} %get-tuple-element.45), channel_id=1, source_target_pairs={{0,1},{1,2},{2,3},{3,4},{4,5},{5,6},{6,7},{8,9},{9,10},{10,11},{11... | collective-permute-start | bytes 983048 | tf_op jit(solution)/shard_map/ppermute | solution.py:300
  164.8 1.7 collective-permute-start.9
  166.5 5.1 %collective-permute-start.12 = (f32[1,160,256]{2,1,0:T(8,128)S(1)}, f32[1,160,256]{2,1,0:T(8,128)S(1)}, u32[]{:S(2)}, u32[]{:S(2)}) collective-permute-start(f32[1,160,256]{2,1,0:T(8,128)S(1)} %collective-permute-done.11), channel_id=1, source_target_pairs={{0,1},{1,2},{2,3},{3,4},{4,5},{5,6},{6,7},{8,9},{9,10},{10,11},{11... | collective-permute-start | bytes 491528 | tf_op jit(solution)/shard_map/ppermute | solution.py:300
  172.2 12.5 %parent_middle.1.middle = f32[16,160,160]{2,1,0:T(8,128)} custom-call(f32[16,160,160]{2,1,0:T(8,128)} %parent_early.1.refs_4_.early, f32[4,160,160]{2,1,0:T(8,128)} %get-tuple-element.42.kept_three, f32[2,160,256]{2,1,0:T(8,128)} %copy-done.6, f32[6,160,256]{2,1,0:T(8,128)} %copy-done.2, f32[1,160,256]{2,1,0:T(8,128)} %copy-done.10, ...), custom_call_target="tpu_custom_call" | custom-call | flops 1800000000 | bytes 10000000 | tf_op jit(solution)/shard_map/parent_middle/pallas_call | solution.py:382
  186.3 6.9 %parent_last.1 = f32[640,640]{1,0:T(8,128)} custom-call(s32[2,2]{1,0:T(2,128)} %counts.1, f32[16,160,160]{2,1,0:T(8,128)} %parent_middle.1.middle, f32[2,160,256]{2,1,0:T(8,128)} %copy-done.8, f32[2,160,256]{2,1,0:T(8,128)} %copy-done.7, f32[1,160,256]{2,1,0:T(8,128)} %copy-done.9), custom_call_target="tpu_custom_call" | custom-call | flops 600000000 | bytes 10000000 | tf_op jit(solution)/shard_map/parent_last/pallas_call | solution.py:394
  194.4 2.5 %collective-permute-done.13 = f32[640,640]{1,0:T(8,128)S(1)} collective-permute-done((f32[640,640]{1,0:T(8,128)}, f32[640,640]{1,0:T(8,128)S(1)}, u32[]{:S(2)}, u32[]{:S(2)}) %collective-permute-start.13) | collective-permute-done | bytes 1638432 | tf_op jit(solution)/shard_map/ppermute | solution.py:305
  196.9 1.6 broadcast_select_fusion
  199.8 36.6 %collective-permute-done.14 = f32[640,640]{1,0:T(8,128)S(1)} collective-permute-done((f32[640,640]{1,0:T(8,128)S(1)}, f32[640,640]{1,0:T(8,128)S(1)}, u32[]{:S(2)}, u32[]{:S(2)}) %collective-permute-start.14) | collective-permute-done | bytes 1638432 | tf_op jit(solution)/shard_map/ppermute | solution.py:305
  236.5 1.3 select_bitcast_fusion
  (48 shorter events, 15.9 us)
Async XLA Ops:
  12.6 26.9 %collective-permute-start = (f32[6,160,256]{2,1,0:T(8,128)}, f32[6,160,256]{2,1,0:T(8,128)S(1)}, u32[]{:S(2)}, u32[]{:S(2)}) collective-permute-start(f32[6,160,256]{2,1,0:T(8,128)} %get-tuple-element.28), channel_id=1, source_target_pairs={{1,0},{2,1},{3,2},{4,3},{5,4},{6,5},{7,6},{9,8},{10,9},{11,10},{12... | collective-permute-start | bytes 2949128 | tf_op jit(solution)/shard_map/ppermute | solution.py:300
  13.9 25.6 %collective-permute-start.1 = (f32[6,160,256]{2,1,0:T(8,128)}, f32[6,160,256]{2,1,0:T(8,128)S(1)}, u32[]{:S(2)}, u32[]{:S(2)}) collective-permute-start(f32[6,160,256]{2,1,0:T(8,128)} %get-tuple-element.29), channel_id=1, source_target_pairs={{8,0},{16,8},{24,16},{9,1},{17,9},{25,17},{10,2},{18,10},{26,18},{... | collective-permute-start | bytes 2949128 | tf_op jit(solution)/shard_map/ppermute | solution.py:300
  39.4 1.0 copy-start.1
  39.4 1.3 copy-start.3
  55.7 8.3 %collective-permute-start.3 = (f32[6,160,256]{2,1,0:T(8,128)}, f32[6,160,256]{2,1,0:T(8,128)S(1)}, u32[]{:S(2)}, u32[]{:S(2)}) collective-permute-start(f32[6,160,256]{2,1,0:T(8,128)} %get-tuple-element.36), channel_id=1, source_target_pairs={{8,0},{16,8},{24,16},{9,1},{17,9},{25,17},{10,2},{18,10},{26,18},{... | collective-permute-start | bytes 2949128 | tf_op jit(solution)/shard_map/ppermute | solution.py:300
  57.0 22.4 %collective-permute-start.2 = (f32[4,160,256]{2,1,0:T(8,128)}, f32[4,160,256]{2,1,0:T(8,128)S(1)}, u32[]{:S(2)}, u32[]{:S(2)}) collective-permute-start(f32[4,160,256]{2,1,0:T(8,128)} %get-tuple-element.35), channel_id=1, source_target_pairs={{0,1},{1,2},{2,3},{3,4},{4,5},{5,6},{6,7},{8,9},{9,10},{10,11},{11... | collective-permute-start | bytes 1966088 | tf_op jit(solution)/shard_map/ppermute | solution.py:300
  62.7 16.7 %collective-permute-start.5 = (f32[4,160,256]{2,1,0:T(8,128)S(1)}, f32[4,160,256]{2,1,0:T(8,128)S(1)}, u32[]{:S(2)}, u32[]{:S(2)}) collective-permute-start(f32[4,160,256]{2,1,0:T(8,128)S(1)} %slice.23), channel_id=1, source_target_pairs={{8,0},{16,8},{24,16},{9,1},{17,9},{25,17},{10,2},{18,10},{26,18},{... | collective-permute-start | bytes 1966088 | tf_op jit(solution)/shard_map/ppermute | solution.py:300
  64.0 15.4 %copy-start = (f32[6,160,256]{2,1,0:T(8,128)}, f32[6,160,256]{2,1,0:T(8,128)S(1)}, u32[]{:S(2)}) copy-start(f32[6,160,256]{2,1,0:T(8,128)S(1)} %collective-permute-done.3.refs_4_.refs_2_) | copy-start | bytes 2949124
  64.1 26.6 %collective-permute-start.4 = (f32[4,160,256]{2,1,0:T(8,128)S(1)}, f32[4,160,256]{2,1,0:T(8,128)S(1)}, u32[]{:S(2)}, u32[]{:S(2)}) collective-permute-start(f32[4,160,256]{2,1,0:T(8,128)S(1)} %bitcast.11), channel_id=1, source_target_pairs={{0,1},{1,2},{2,3},{3,4},{4,5},{5,6},{6,7},{8,9},{9,10},{10,11},{11... | collective-permute-start | bytes 1966088 | tf_op jit(solution)/shard_map/ppermute | solution.py:300
  79.4 11.3 %copy-start.4 = (f32[4,160,256]{2,1,0:T(8,128)}, f32[4,160,256]{2,1,0:T(8,128)S(1)}, u32[]{:S(2)}) copy-start(f32[4,160,256]{2,1,0:T(8,128)S(1)} %collective-permute-done.2.refs_3_.refs_2_) | copy-start | bytes 1966084
  79.4 11.3 %copy-start.5 = (f32[4,160,256]{2,1,0:T(8,128)}, f32[4,160,256]{2,1,0:T(8,128)S(1)}, u32[]{:S(2)}) copy-start(f32[4,160,256]{2,1,0:T(8,128)S(1)} %collective-permute-done.5.refs_6_.refs_1_) | copy-start | bytes 1966084
  90.7 0.8 copy-start.12
  108.7 28.4 %collective-permute-start.6 = (f32[6,160,256]{2,1,0:T(8,128)}, f32[6,160,256]{2,1,0:T(8,128)S(1)}, u32[]{:S(2)}, u32[]{:S(2)}) collective-permute-start(f32[6,160,256]{2,1,0:T(8,128)} %get-tuple-element.40), channel_id=1, source_target_pairs={{1,0},{2,1},{3,2},{4,3},{5,4},{6,5},{7,6},{9,8},{10,9},{11,10},{12... | collective-permute-start | bytes 2949128 | tf_op jit(solution)/shard_map/ppermute | solution.py:300
  110.0 27.0 %collective-permute-start.7 = (f32[2,160,256]{2,1,0:T(8,128)}, f32[2,160,256]{2,1,0:T(8,128)S(1)}, u32[]{:S(2)}, u32[]{:S(2)}) collective-permute-start(f32[2,160,256]{2,1,0:T(8,128)} %get-tuple-element.41), channel_id=1, source_target_pairs={{0,8},{8,16},{16,24},{1,9},{9,17},{17,25},{2,10},{10,18},{18,26},{... | collective-permute-start | bytes 983048 | tf_op jit(solution)/shard_map/ppermute | solution.py:300
  137.8 1.0 copy-start.2
  153.4 13.1 %collective-permute-start.11 = (f32[1,160,256]{2,1,0:T(8,128)}, f32[1,160,256]{2,1,0:T(8,128)S(1)}, u32[]{:S(2)}, u32[]{:S(2)}) collective-permute-start(f32[1,160,256]{2,1,0:T(8,128)} %get-tuple-element.46), channel_id=1, source_target_pairs={{0,8},{8,16},{16,24},{1,9},{9,17},{17,25},{2,10},{10,18},{18,26},{... | collective-permute-start | bytes 491528 | tf_op jit(solution)/shard_map/ppermute | solution.py:300
  157.8 13.7 %collective-permute-start.8 = (f32[1,160,256]{2,1,0:T(8,128)S(1)}, f32[1,160,256]{2,1,0:T(8,128)S(1)}, u32[]{:S(2)}, u32[]{:S(2)}) collective-permute-start(f32[1,160,256]{2,1,0:T(8,128)S(1)} %slice.24), channel_id=1, source_target_pairs={{0,8},{8,16},{16,24},{1,9},{9,17},{17,25},{2,10},{10,18},{18,26},{... | collective-permute-start | bytes 491528 | tf_op jit(solution)/shard_map/ppermute | solution.py:300
  159.8 25.0 %collective-permute-start.10 = (f32[2,160,256]{2,1,0:T(8,128)}, f32[2,160,256]{2,1,0:T(8,128)S(1)}, u32[]{:S(2)}, u32[]{:S(2)}) collective-permute-start(f32[2,160,256]{2,1,0:T(8,128)} %get-tuple-element.45), channel_id=1, source_target_pairs={{0,1},{1,2},{2,3},{3,4},{4,5},{5,6},{6,7},{8,9},{9,10},{10,11},{11... | collective-permute-start | bytes 983048 | tf_op jit(solution)/shard_map/ppermute | solution.py:300
  164.8 20.0 %collective-permute-start.9 = (f32[2,160,256]{2,1,0:T(8,128)}, f32[2,160,256]{2,1,0:T(8,128)S(1)}, u32[]{:S(2)}, u32[]{:S(2)}) collective-permute-start(f32[2,160,256]{2,1,0:T(8,128)} %get-tuple-element.44), channel_id=1, source_target_pairs={{0,8},{8,16},{16,24},{1,9},{9,17},{17,25},{2,10},{10,18},{18,26},{... | collective-permute-start | bytes 983048 | tf_op jit(solution)/shard_map/ppermute | solution.py:300
  166.5 18.3 %collective-permute-start.12 = (f32[1,160,256]{2,1,0:T(8,128)S(1)}, f32[1,160,256]{2,1,0:T(8,128)S(1)}, u32[]{:S(2)}, u32[]{:S(2)}) collective-permute-start(f32[1,160,256]{2,1,0:T(8,128)S(1)} %collective-permute-done.11), channel_id=1, source_target_pairs={{0,1},{1,2},{2,3},{3,4},{4,5},{5,6},{6,7},{8,9},{9,10},{10,11},{11... | collective-permute-start | bytes 491528 | tf_op jit(solution)/shard_map/ppermute | solution.py:300
  184.8 8.4 %copy-start.11 = (s32[1,1,2]{2,1,0:T(1,128)S(1)}, s32[1,1,2]{2,1,0:T(1,128)}, u32[]{:S(2)}) copy-start(s32[1,1,2]{2,1,0:T(1,128)} %param.7) | copy-start | bytes 28
  184.8 0.8 copy-start.7
  193.2 3.7 %collective-permute-start.13 = (f32[640,640]{1,0:T(8,128)}, f32[640,640]{1,0:T(8,128)S(1)}, u32[]{:S(2)}, u32[]{:S(2)}) collective-permute-start(f32[640,640]{1,0:T(8,128)} %parent_last.1), channel_id=1, source_target_pairs={{0,8},{8,0},{16,24},{24,16},{1,9},{9,1},{17,25},{25,17},{2,10},{10... | collective-permute-start | bytes 4915208 | tf_op jit(solution)/shard_map/ppermute | solution.py:305
  198.6 37.9 %collective-permute-start.14 = (f32[640,640]{1,0:T(8,128)S(1)}, f32[640,640]{1,0:T(8,128)S(1)}, u32[]{:S(2)}, u32[]{:S(2)}) collective-permute-start(f32[640,640]{1,0:T(8,128)S(1)} %broadcast_select_fusion), channel_id=1, source_target_pairs={{0,1},{1,0},{2,3},{3,2},{4,5},{5,4},{6,7},{7,6},{8,9},{9,8},{10,11... | collective-permute-start | bytes 4915208 | tf_op jit(solution)/shard_map/ppermute | solution.py:305
  (4 other events, 2.8 us)

commit v3 on v2

--- a/solution.py
+++ b/solution.py
@@ -106,7 +106,7 @@
     return copy
 
 
-def eliminate_kernel(home, base_at, sources, rects_out, keep, n_extra, *refs):
+def eliminate_kernel(home, base_at, sources, rects_out, keep, n_extra, relay, *refs):
     n_src, n_out = len(sources), len(rects_out)
     counts, base, interp_all = refs[:3]
     src = refs[3 : 3 + n_src]
@@ -119,6 +119,8 @@
     low = points - slots
     first = load(base, base_at, store, sems.at[0])
     second = load(interp_all, (home[0], home[1]), interp, sems.at[1])
+    if relay is not None:
+        outs[1][outs[1].shape[0] - 1] = src[0][relay]
     first.wait()
     second.wait()
     for ref, (rect, target) in zip(src, sources):
@@ -169,20 +171,25 @@
     )
 
 
-def eliminate(home, counts, base, base_at, interp, sources, rects_out, keep, extra=()):
+def eliminate(home, counts, base, base_at, interp, sources, rects_out, keep, extra=(), relay=None):
     points, slots = base.shape[-1], interp.shape[-1]
     rects_out = [FULL] + list(rects_out)
     out_shape = [
         jax.ShapeDtypeStruct(
-            ((r[1] - r[0] + 1) * (r[3] - r[2] + 1), slots, points), jnp.float32
+            (
+                (r[1] - r[0] + 1) * (r[3] - r[2] + 1) + (relay is not None and at == 1),
+                slots,
+                points,
+            ),
+            jnp.float32,
         )
-        for r in rects_out
+        for at, r in enumerate(rects_out)
     ]
     if keep:
         out_shape.append(jax.ShapeDtypeStruct((4, slots, slots), jnp.float32))
     plan = [(rect, target) for _, rect, target in sources]
     return pl.pallas_call(
-        functools.partial(eliminate_kernel, home, base_at, plan, rects_out, keep, len(extra)),
+        functools.partial(eliminate_kernel, home, base_at, plan, rects_out, keep, len(extra), relay),
         out_shape=out_shape,
         in_specs=[SMEM, ANY, ANY] + [VMEM] * len(sources) + [ANY] * len(extra),
         out_specs=[VMEM] * len(out_shape),
@@ -284,6 +291,8 @@
         acc[i] = middle[i]
     for ref, (rect, shift, colour) in zip(src, plan):
         parent_apply(acc, ref, rect, shift, colour)
+    relayed = src[0][3]
+    acc[5] = acc[5] - product(split(relayed.T[low:]), split(relayed[:, low:]))
     row_ids = lax.broadcasted_iota(jnp.int32, (slots, slots), 0) + low
     col_ids = lax.broadcasted_iota(jnp.int32, (slots, slots), 1) + low
     for x in range(4):
@@ -312,7 +321,7 @@
     left0, up0, diag0 = (-1, 1, -1, 0), (-1, 0, -1, 1), (-1, 0, -1, 0)
     right1, up1, diag1 = (0, 1, 0, 1), (-1, 0, -1, 1), (-1, 0, 0, 1)
     left2, down2 = (-1, 1, -1, 0), (1, 1, 0, 1)
-    down3, right3 = (1, 1, -1, 0), (-1, 0, 1, 1)
+    down3, right3 = (1, 1, -1, 1), (-1, 0, 1, 1)
     corner3 = (1, 1, 1, 1)
 
     w0, l0, u0 = eliminate(
@@ -333,22 +342,24 @@
     u1 = send(u1, "row", -1)
     d1 = send(u1.reshape(2, 3, slots, points)[:, 1:].reshape(4, slots, points), "col", 1)
     acc2, acc3 = update(
-        "gap_one", [acc2, acc3], [u0, w1, l0],
+        "gap_one", [acc2, acc3], [u0, w1, l0, u1],
         [
-            (0, None, [(0, up0, (-1, 0)), (1, FULL, (1, -1))]),
-            (1, None, [(0, up0, (-1, 1)), (1, FULL, (1, 0)), (2, left0, (1, -1))]),
+            (0, None, [(0, up0, (-1, 0)), (1, FULL, (1, -1)), (3, up1, (-1, -1))]),
+            (1, None, [
+                (0, up0, (-1, 1)), (1, FULL, (1, 0)), (2, left0, (1, -1)), (3, up1, (-1, 0)),
+            ]),
         ],
     )
     w2, l2, v2, kept2 = eliminate(
         (1, 0), red_count, acc2, None, interp,
-        [(r1, right1, (1, 1)), (u1, up1, (-1, -1)), (d1, diag1, (-1, 1))],
+        [(r1, right1, (1, 1)), (d1, diag1, (-1, 1))],
         [left2, down2], True, extra=(d0,),
     )
     l2 = send(l2, "col", -1)
     v2 = send(v2, "row", 1)
     (acc3,) = update(
-        "gap_two", [acc3], [d0, u1, w2],
-        [(0, None, [(0, diag0, (-1, -1)), (1, up1, (-1, 0)), (2, FULL, (0, 1))])],
+        "gap_two", [acc3], [d0, w2],
+        [(0, None, [(0, diag0, (-1, -1)), (1, FULL, (0, 1))])],
     )
     plan_early = [
         (w0, FULL, (0, 0), 0), (w1, FULL, (0, 1), 1), (r1, right1, (0, -1), 1),
@@ -366,18 +377,17 @@
         cost_estimate=cost(30),
         name="parent_early",
     )(boxes, kept1, kept2, *[entry[0] for entry in plan_early])
-    w3, v3, r3, d3, kept3 = eliminate(
+    w3, v3, r3, kept3 = eliminate(
         (1, 1), red_count, acc3, None, interp, [(l2, left2, (0, -1))],
-        [down3, right3, corner3], True, extra=(early, v2),
+        [down3, right3], True, extra=(early, v2), relay=4,
     )
     v3 = send(v3, "row", 1)
     r3 = send(r3, "col", 1)
-    d3 = send(send(d3, "row", 1), "col", 1)
-    d2 = send(l2[4:5], "row", 1)
+    d3 = send(v3[2:3], "col", 1)
 
     plan_middle = [
         (v2, down2, (-1, 0), 2), (l2, left2, (1, 2), 2),
-        (d2, (1, 1, -1, -1), (-1, 2), 2), (w3, FULL, (1, 1), 3),
+        (w3, FULL, (1, 1), 3),
     ]
     middle = pl.pallas_call(
         functools.partial(parent_middle_kernel, [entry[1:] for entry in plan_middle]),

time: 239 us -> 234 us (0.979)
  waiting for transfers between devices: 64.4 us -> 59.7 us
    ppermute x2, starting transfers between devices: 0.67 us -> 5.64 us  [from_partner(): return lax.ppermute(value, axis, pairs)]
    ppermute x13 -> x11, starting transfers between devices: 33.5 us -> 29.9 us  [send(): return lax.ppermute(value, axis, pairs)]
    ppermute x13 -> x11, waiting for transfers between devices: 25.2 us -> 22 us  [send(): return lax.ppermute(value, axis, pairs)]
    unnamed x26 -> x24, local copies, waits for them, and re-layouts: 5.99 us -> 5.28 us
  transfers between devices with their start and end apart: 15 -> 13, of which waited for: 4 -> 4; matrix products, arithmetic and copies ran while one was open for 1% -> 1% of each run, Pallas kernels for 25% -> 26%
where the time goes in v3:
time: 234 us; the launch traced here: 233 us
  Pallas kernels  126 us (54%)
  waiting for transfers between devices  59.7 us (26%)
  starting transfers between devices  35.6 us (15%)
  local copies, waits for them, and re-layouts  7.14 us (3%)
  other arithmetic  2.98 us (1%)
    pallas_call x4, Pallas kernels, eliminate(): pl.pallas_call(functools.partial(eliminate_kernel, home, base_at, plan, r...  57.9 us
    ppermute x2, waiting for transfers between devices, from_partner(): return lax.ppermute(value, axis, pairs)  37.7 us
    pallas_call x3, Pallas kernels, update(): pl.pallas_call(functools.partial(update_kernel, jobs, len(bases), len(sou...  33.7 us
    ppermute x11, starting transfers between devices, send(): return lax.ppermute(value, axis, pairs)  29.9 us
    ppermute x11, waiting for transfers between devices, send(): return lax.ppermute(value, axis, pairs)  22 us
    pallas_call x1, Pallas kernels, local(): pl.pallas_call(functools.partial(parent_early_kernel, [entry[1:] for entr...  14.9 us
    pallas_call x1, Pallas kernels, local(): pl.pallas_call(functools.partial(parent_middle_kernel, [entry[1:] for ent...  12.3 us
    pallas_call x1, Pallas kernels, local(): pl.pallas_call(functools.partial(parent_last_kernel, [entry[1:] for entry...  7.24 us
  transfers between devices with their start and end apart: 13, of which 4 were waited for; matrix products, arithmetic and copies ran while one was open for 1% of the time, Pallas kernels for 26%

profile of v3, /device:TPU:0, one launch (start us, length us, event | category | flops | bytes accessed | tf_op | source)
XLA Modules:
  0.0 233.0 jit_solution(4056326097515204349)
XLA Ops:
  0.0 12.6 %eliminate_00.1 = (f32[9,160,256]{2,1,0:T(8,128)}, f32[6,160,256]{2,1,0:T(8,128)}, f32[6,160,256]{2,1,0:T(8,128)}) custom-call(s32[2,2]{1,0:T(2,128)} %counts.1, f32[4,9,256,256]{3,2,1,0:T(8,128)} %bitcast.7, f32[2,2,160,160]{3,2,1,0:T(8,128)} %refs_2_.7), custom_call_target="tpu_custom_call" | custom-call | flops 3600000000 | bytes 10000000 | tf_op jit(solution)/shard_map/eliminate_00/pallas_call | solution.py:191
  15.2 10.3 %gap_zero.1 = (f32[9,256,256]{2,1,0:T(8,128)}, f32[9,256,256]{2,1,0:T(8,128)}, f32[9,256,256]{2,1,0:T(8,128)}) custom-call(f32[4,9,256,256]{3,2,1,0:T(8,128)} %bitcast.8, f32[9,160,256]{2,1,0:T(8,128)} %get-tuple-element.25.refs_1_.refs_0_), custom_call_target="tpu_custom_call" | custom-call | flops 1200000000 | bytes 10000000 | tf_op jit(solution)/shard_map/gap_zero/pallas_call | solution.py:222
  25.5 13.9 %collective-permute-done.refs_3_.refs_4_ = f32[6,160,256]{2,1,0:T(8,128)S(1)} collective-permute-done((f32[6,160,256]{2,1,0:T(8,128)}, f32[6,160,256]{2,1,0:T(8,128)S(1)}, u32[]{:S(2)}, u32[]{:S(2)}) %collective-permute-start) | collective-permute-done | bytes 983072 | tf_op jit(solution)/shard_map/ppermute | solution.py:309
  40.8 15.0 %eliminate_01.1 = (f32[9,160,256]{2,1,0:T(8,128)}, f32[4,160,256]{2,1,0:T(8,128)}, f32[6,160,256]{2,1,0:T(8,128)}, f32[4,160,160]{2,1,0:T(8,128)}) custom-call(s32[2,2]{1,0:T(2,128)} %counts.1, f32[9,256,256]{2,1,0:T(8,128)} %get-tuple-element.26.refs_1_, f32[2,2,160,160]{3,2,1,0:T(8,128)} %refs_2_.7, f32[6,160,256]{2,1,0:T(8,128)} %copy-done, ...), custom_call_target="tpu_custom_call" | custom-call | flops 3600000000 | bytes 10000000 | tf_op jit(solution)/shard_map/eliminate_01/pallas_call | solution.py:191
  57.1 4.6 %collective-permute-start.3 = (f32[4,160,256]{2,1,0:T(8,128)}, f32[4,160,256]{2,1,0:T(8,128)S(1)}, u32[]{:S(2)}, u32[]{:S(2)}) collective-permute-start(f32[4,160,256]{2,1,0:T(8,128)} %get-tuple-element.35), channel_id=1, source_target_pairs={{0,1},{1,2},{2,3},{3,4},{4,5},{5,6},{6,7},{8,9},{9,10},{10,11},{11... | collective-permute-start | bytes 1966088 | tf_op jit(solution)/shard_map/ppermute | solution.py:309
  64.2 2.7 %collective-permute-start.4 = (f32[4,160,256]{2,1,0:T(8,128)S(1)}, f32[4,160,256]{2,1,0:T(8,128)S(1)}, u32[]{:S(2)}, u32[]{:S(2)}) collective-permute-start(f32[4,160,256]{2,1,0:T(8,128)S(1)} %bitcast.11), channel_id=1, source_target_pairs={{0,1},{1,2},{2,3},{3,4},{4,5},{5,6},{6,7},{8,9},{9,10},{10,11},{11... | collective-permute-start | bytes 1966088 | tf_op jit(solution)/shard_map/ppermute | solution.py:309
  66.9 15.8 %gap_one.1 = (f32[9,256,256]{2,1,0:T(8,128)}, f32[9,256,256]{2,1,0:T(8,128)}) custom-call(f32[9,256,256]{2,1,0:T(8,128)} %get-tuple-element.30.refs_0_, f32[9,256,256]{2,1,0:T(8,128)} %get-tuple-element.31.refs_1_, f32[6,160,256]{2,1,0:T(8,128)} %copy-done.4, f32[9,160,256]{2,1,0:T(8,128)} %get-tuple-element.32.refs_3_.refs_1_, f32[6,160,256]{2,1,0:T(8,128)} %copy-done, ...), custom_call_target="tpu_custom_call" | custom-call | flops 1200000000 | bytes 10000000 | tf_op jit(solution)/shard_map/gap_one/pallas_call | solution.py:222
  82.7 8.1 %collective-permute-done.4.refs_4_ = f32[4,160,256]{2,1,0:T(8,128)S(1)} collective-permute-done((f32[4,160,256]{2,1,0:T(8,128)S(1)}, f32[4,160,256]{2,1,0:T(8,128)S(1)}, u32[]{:S(2)}, u32[]{:S(2)}) %collective-permute-start.4) | collective-permute-done | bytes 655392 | tf_op jit(solution)/shard_map/ppermute | solution.py:309
  91.7 15.6 %eliminate_10.1 = (f32[9,160,256]{2,1,0:T(8,128)}, f32[6,160,256]{2,1,0:T(8,128)}, f32[2,160,256]{2,1,0:T(8,128)}, f32[4,160,160]{2,1,0:T(8,128)}) custom-call(s32[2,2]{1,0:T(2,128)} %counts.1, f32[9,256,256]{2,1,0:T(8,128)} %get-tuple-element.34.refs_1_, f32[2,2,160,160]{3,2,1,0:T(8,128)} %refs_2_.7, f32[4,160,256]{2,1,0:T(8,128)} %copy-done.5, ...), custom_call_target="tpu_custom_call" | custom-call | flops 3600000000 | bytes 10000000 | tf_op jit(solution)/shard_map/eliminate_10/pallas_call | solution.py:191
  108.6 3.7 %collective-permute-start.7 = (f32[2,160,256]{2,1,0:T(8,128)}, f32[2,160,256]{2,1,0:T(8,128)S(1)}, u32[]{:S(2)}, u32[]{:S(2)}) collective-permute-start(f32[2,160,256]{2,1,0:T(8,128)} %get-tuple-element.40), channel_id=1, source_target_pairs={{0,8},{8,16},{16,24},{1,9},{9,17},{17,25},{2,10},{10,18},{18,26},{... | collective-permute-start | bytes 983048 | tf_op jit(solution)/shard_map/ppermute | solution.py:309
  112.3 7.6 %gap_two.1.refs_1_ = f32[9,256,256]{2,1,0:T(8,128)} custom-call(f32[9,256,256]{2,1,0:T(8,128)} %get-tuple-element.38.refs_0_, f32[4,160,256]{2,1,0:T(8,128)} %copy-done.6, f32[9,160,256]{2,1,0:T(8,128)} %get-tuple-element.37.refs_3_.refs_2_), custom_call_target="tpu_custom_call" | custom-call | flops 1200000000 | bytes 10000000 | tf_op jit(solution)/shard_map/gap_two/pallas_call | solution.py:222
  119.9 14.9 %parent_early.1.refs_4_.early = f32[16,160,160]{2,1,0:T(8,128)} custom-call(f32[4,9,256,256]{3,2,1,0:T(8,128)} %bitcast.9, f32[4,160,160]{2,1,0:T(8,128)} %get-tuple-element.29.kept_one, f32[4,160,160]{2,1,0:T(8,128)} %get-tuple-element.36.kept_two, f32[9,160,256]{2,1,0:T(8,128)} %get-tuple-element.25.refs_1_.refs_0_, ...), custom_call_target="tpu_custom_call" | custom-call | flops 1800000000 | bytes 10000000 | tf_op jit(solution)/shard_map/parent_early/pallas_call | solution.py:368
  136.5 14.8 %eliminate_11.1 = (f32[9,160,256]{2,1,0:T(8,128)}, f32[4,160,256]{2,1,0:T(8,128)}, f32[2,160,256]{2,1,0:T(8,128)}, f32[4,160,160]{2,1,0:T(8,128)}) custom-call(s32[2,2]{1,0:T(2,128)} %counts.1, f32[9,256,256]{2,1,0:T(8,128)} %gap_two.1.refs_1_, f32[2,2,160,160]{3,2,1,0:T(8,128)} %refs_2_.7, f32[6,160,256]{2,1,0:T(8,128)} %copy-done.3, ...), custom_call_target="tpu_custom_call" | custom-call | flops 3600000000 | bytes 10000000 | tf_op jit(solution)/shard_map/eliminate_11/pallas_call | solution.py:191
  151.3 2.4 %collective-permute-start.8 = (f32[4,160,256]{2,1,0:T(8,128)}, f32[4,160,256]{2,1,0:T(8,128)S(1)}, u32[]{:S(2)}, u32[]{:S(2)}) collective-permute-start(f32[4,160,256]{2,1,0:T(8,128)} %get-tuple-element.43), channel_id=1, source_target_pairs={{0,8},{8,16},{16,24},{1,9},{9,17},{17,25},{2,10},{10,18},{18,26},{... | collective-permute-start | bytes 1966088 | tf_op jit(solution)/shard_map/ppermute | solution.py:309
  153.6 5.0 %collective-permute-start.9 = (f32[2,160,256]{2,1,0:T(8,128)}, f32[2,160,256]{2,1,0:T(8,128)S(1)}, u32[]{:S(2)}, u32[]{:S(2)}) collective-permute-start(f32[2,160,256]{2,1,0:T(8,128)} %get-tuple-element.44), channel_id=1, source_target_pairs={{0,1},{1,2},{2,3},{3,4},{4,5},{5,6},{6,7},{8,9},{9,10},{10,11},{11... | collective-permute-start | bytes 983048 | tf_op jit(solution)/shard_map/ppermute | solution.py:309
  158.7 5.1 %collective-permute-start.10 = (f32[1,160,256]{2,1,0:T(8,128)S(1)}, f32[1,160,256]{2,1,0:T(8,128)S(1)}, u32[]{:S(2)}, u32[]{:S(2)}) collective-permute-start(f32[1,160,256]{2,1,0:T(8,128)S(1)} %slice.24), channel_id=1, source_target_pairs={{0,1},{1,2},{2,3},{3,4},{4,5},{5,6},{6,7},{8,9},{9,10},{10,11},{11... | collective-permute-start | bytes 491528 | tf_op jit(solution)/shard_map/ppermute | solution.py:309
  163.8 12.3 %parent_middle.1.middle = f32[16,160,160]{2,1,0:T(8,128)} custom-call(f32[16,160,160]{2,1,0:T(8,128)} %parent_early.1.refs_4_.early, f32[4,160,160]{2,1,0:T(8,128)} %get-tuple-element.41.kept_three, f32[2,160,256]{2,1,0:T(8,128)} %copy-done.7, f32[6,160,256]{2,1,0:T(8,128)} %copy-done.3, f32[9,160,256]{2,1,0:T(8,128)} %get-tuple-element.42.refs_2_), custom_call_target="tpu_custom_call" | custom-call | flops 1800000000 | bytes 10000000 | tf_op jit(solution)/shard_map/parent_middle/pallas_call | solution.py:392
  177.5 7.2 %parent_last.1 = f32[640,640]{1,0:T(8,128)} custom-call(s32[2,2]{1,0:T(2,128)} %counts.1, f32[16,160,160]{2,1,0:T(8,128)} %parent_middle.1.middle, f32[4,160,256]{2,1,0:T(8,128)} %copy-done.2, f32[2,160,256]{2,1,0:T(8,128)} %copy-done.8, f32[1,160,256]{2,1,0:T(8,128)} %copy-done.9), custom_call_target="tpu_custom_call" | custom-call | flops 600000000 | bytes 10000000 | tf_op jit(solution)/shard_map/parent_last/pallas_call | solution.py:404
  184.7 2.7 %collective-permute-start.11 = (f32[640,640]{1,0:T(8,128)}, f32[640,640]{1,0:T(8,128)S(1)}, u32[]{:S(2)}, u32[]{:S(2)}) collective-permute-start(f32[640,640]{1,0:T(8,128)} %parent_last.1), channel_id=1, source_target_pairs={{0,8},{8,0},{16,24},{24,16},{1,9},{9,1},{17,25},{25,17},{2,10},{10... | collective-permute-start | bytes 4915208 | tf_op jit(solution)/shard_map/ppermute | solution.py:314
  188.6 2.1 collective-permute-done.11
  190.7 1.6 broadcast_select_fusion
  192.4 3.0 %collective-permute-start.12 = (f32[640,640]{1,0:T(8,128)S(1)}, f32[640,640]{1,0:T(8,128)S(1)}, u32[]{:S(2)}, u32[]{:S(2)}) collective-permute-start(f32[640,640]{1,0:T(8,128)S(1)} %broadcast_select_fusion), channel_id=1, source_target_pairs={{0,1},{1,0},{2,3},{3,2},{4,5},{5,4},{6,7},{7,6},{8,9},{9,8},{10,11... | collective-permute-start | bytes 4915208 | tf_op jit(solution)/shard_map/ppermute | solution.py:314
  196.1 35.6 %collective-permute-done.12 = f32[640,640]{1,0:T(8,128)S(1)} collective-permute-done((f32[640,640]{1,0:T(8,128)S(1)}, f32[640,640]{1,0:T(8,128)S(1)}, u32[]{:S(2)}, u32[]{:S(2)}) %collective-permute-start.12) | collective-permute-done | bytes 1638432 | tf_op jit(solution)/shard_map/ppermute | solution.py:314
  231.7 1.3 select_bitcast_fusion
  (42 shorter events, 13.6 us)
Async XLA Ops:
  12.6 26.9 %collective-permute-start = (f32[6,160,256]{2,1,0:T(8,128)}, f32[6,160,256]{2,1,0:T(8,128)S(1)}, u32[]{:S(2)}, u32[]{:S(2)}) collective-permute-start(f32[6,160,256]{2,1,0:T(8,128)} %get-tuple-element.27), channel_id=1, source_target_pairs={{1,0},{2,1},{3,2},{4,3},{5,4},{6,5},{7,6},{9,8},{10,9},{11,10},{12... | collective-permute-start | bytes 2949128 | tf_op jit(solution)/shard_map/ppermute | solution.py:309
  13.9 25.6 %collective-permute-start.1 = (f32[6,160,256]{2,1,0:T(8,128)}, f32[6,160,256]{2,1,0:T(8,128)S(1)}, u32[]{:S(2)}, u32[]{:S(2)}) collective-permute-start(f32[6,160,256]{2,1,0:T(8,128)} %get-tuple-element.28), channel_id=1, source_target_pairs={{8,0},{16,8},{24,16},{9,1},{17,9},{25,17},{10,2},{18,10},{26,18},{... | collective-permute-start | bytes 2949128 | tf_op jit(solution)/shard_map/ppermute | solution.py:309
  39.4 0.9 copy-start
  39.4 1.4 copy-start.4
  55.8 8.3 %collective-permute-start.2 = (f32[6,160,256]{2,1,0:T(8,128)}, f32[6,160,256]{2,1,0:T(8,128)S(1)}, u32[]{:S(2)}, u32[]{:S(2)}) collective-permute-start(f32[6,160,256]{2,1,0:T(8,128)} %get-tuple-element.33), channel_id=1, source_target_pairs={{8,0},{16,8},{24,16},{9,1},{17,9},{25,17},{10,2},{18,10},{26,18},{... | collective-permute-start | bytes 2949128 | tf_op jit(solution)/shard_map/ppermute | solution.py:309
  57.1 25.6 %collective-permute-start.3 = (f32[4,160,256]{2,1,0:T(8,128)}, f32[4,160,256]{2,1,0:T(8,128)S(1)}, u32[]{:S(2)}, u32[]{:S(2)}) collective-permute-start(f32[4,160,256]{2,1,0:T(8,128)} %get-tuple-element.35), channel_id=1, source_target_pairs={{0,1},{1,2},{2,3},{3,4},{4,5},{5,6},{6,7},{8,9},{9,10},{10,11},{11... | collective-permute-start | bytes 1966088 | tf_op jit(solution)/shard_map/ppermute | solution.py:309
  62.8 19.9 %collective-permute-start.5 = (f32[4,160,256]{2,1,0:T(8,128)S(1)}, f32[4,160,256]{2,1,0:T(8,128)S(1)}, u32[]{:S(2)}, u32[]{:S(2)}) collective-permute-start(f32[4,160,256]{2,1,0:T(8,128)S(1)} %slice.23), channel_id=1, source_target_pairs={{8,0},{16,8},{24,16},{9,1},{17,9},{25,17},{10,2},{18,10},{26,18},{... | collective-permute-start | bytes 1966088 | tf_op jit(solution)/shard_map/ppermute | solution.py:309
  64.1 2.8 %copy-start.1 = (f32[6,160,256]{2,1,0:T(8,128)}, f32[6,160,256]{2,1,0:T(8,128)S(1)}, u32[]{:S(2)}) copy-start(f32[6,160,256]{2,1,0:T(8,128)S(1)} %collective-permute-done.2.refs_5_) | copy-start | bytes 2949124
  64.2 26.6 %collective-permute-start.4 = (f32[4,160,256]{2,1,0:T(8,128)S(1)}, f32[4,160,256]{2,1,0:T(8,128)S(1)}, u32[]{:S(2)}, u32[]{:S(2)}) collective-permute-start(f32[4,160,256]{2,1,0:T(8,128)S(1)} %bitcast.11), channel_id=1, source_target_pairs={{0,1},{1,2},{2,3},{3,4},{4,5},{5,6},{6,7},{8,9},{9,10},{10,11},{11... | collective-permute-start | bytes 1966088 | tf_op jit(solution)/shard_map/ppermute | solution.py:309
  82.7 8.1 %copy-start.5 = (f32[4,160,256]{2,1,0:T(8,128)}, f32[4,160,256]{2,1,0:T(8,128)S(1)}, u32[]{:S(2)}) copy-start(f32[4,160,256]{2,1,0:T(8,128)S(1)} %collective-permute-done.3.refs_3_.refs_2_) | copy-start | bytes 1966084
  82.7 8.1 %copy-start.6 = (f32[4,160,256]{2,1,0:T(8,128)}, f32[4,160,256]{2,1,0:T(8,128)S(1)}, u32[]{:S(2)}) copy-start(f32[4,160,256]{2,1,0:T(8,128)S(1)} %collective-permute-done.5.refs_5_.refs_1_) | copy-start | bytes 1966084
  90.8 0.8 copy-start.11
  107.3 27.5 %collective-permute-start.6 = (f32[6,160,256]{2,1,0:T(8,128)}, f32[6,160,256]{2,1,0:T(8,128)S(1)}, u32[]{:S(2)}, u32[]{:S(2)}) collective-permute-start(f32[6,160,256]{2,1,0:T(8,128)} %get-tuple-element.39), channel_id=1, source_target_pairs={{1,0},{2,1},{3,2},{4,3},{5,4},{6,5},{7,6},{9,8},{10,9},{11,10},{12... | collective-permute-start | bytes 2949128 | tf_op jit(solution)/shard_map/ppermute | solution.py:309
  108.6 26.2 %collective-permute-start.7 = (f32[2,160,256]{2,1,0:T(8,128)}, f32[2,160,256]{2,1,0:T(8,128)S(1)}, u32[]{:S(2)}, u32[]{:S(2)}) collective-permute-start(f32[2,160,256]{2,1,0:T(8,128)} %get-tuple-element.40), channel_id=1, source_target_pairs={{0,8},{8,16},{16,24},{1,9},{9,17},{17,25},{2,10},{10,18},{18,26},{... | collective-permute-start | bytes 983048 | tf_op jit(solution)/shard_map/ppermute | solution.py:309
  134.8 0.7 copy-start.7
  135.5 1.0 copy-start.3
  151.3 7.4 %collective-permute-start.8 = (f32[4,160,256]{2,1,0:T(8,128)}, f32[4,160,256]{2,1,0:T(8,128)S(1)}, u32[]{:S(2)}, u32[]{:S(2)}) collective-permute-start(f32[4,160,256]{2,1,0:T(8,128)} %get-tuple-element.43), channel_id=1, source_target_pairs={{0,8},{8,16},{16,24},{1,9},{9,17},{17,25},{2,10},{10,18},{18,26},{... | collective-permute-start | bytes 1966088 | tf_op jit(solution)/shard_map/ppermute | solution.py:309
  153.6 22.4 %collective-permute-start.9 = (f32[2,160,256]{2,1,0:T(8,128)}, f32[2,160,256]{2,1,0:T(8,128)S(1)}, u32[]{:S(2)}, u32[]{:S(2)}) collective-permute-start(f32[2,160,256]{2,1,0:T(8,128)} %get-tuple-element.44), channel_id=1, source_target_pairs={{0,1},{1,2},{2,3},{3,4},{4,5},{5,6},{6,7},{8,9},{9,10},{10,11},{11... | collective-permute-start | bytes 983048 | tf_op jit(solution)/shard_map/ppermute | solution.py:309
  158.7 17.4 %copy-start.2 = (f32[4,160,256]{2,1,0:T(8,128)}, f32[4,160,256]{2,1,0:T(8,128)S(1)}, u32[]{:S(2)}) copy-start(f32[4,160,256]{2,1,0:T(8,128)S(1)} %collective-permute-done.8.refs_0_) | copy-start | bytes 1966084
  158.7 17.4 %collective-permute-start.10 = (f32[1,160,256]{2,1,0:T(8,128)S(1)}, f32[1,160,256]{2,1,0:T(8,128)S(1)}, u32[]{:S(2)}, u32[]{:S(2)}) collective-permute-start(f32[1,160,256]{2,1,0:T(8,128)S(1)} %slice.24), channel_id=1, source_target_pairs={{0,1},{1,2},{2,3},{3,4},{4,5},{5,6},{6,7},{8,9},{9,10},{10,11},{11... | collective-permute-start | bytes 491528 | tf_op jit(solution)/shard_map/ppermute | solution.py:309
  176.1 11.3 %copy-start.10 = (s32[1,1,2]{2,1,0:T(1,128)S(1)}, s32[1,1,2]{2,1,0:T(1,128)}, u32[]{:S(2)}) copy-start(s32[1,1,2]{2,1,0:T(1,128)} %param.7) | copy-start | bytes 28
  176.1 0.7 copy-start.8
  184.7 6.0 %collective-permute-start.11 = (f32[640,640]{1,0:T(8,128)}, f32[640,640]{1,0:T(8,128)S(1)}, u32[]{:S(2)}, u32[]{:S(2)}) collective-permute-start(f32[640,640]{1,0:T(8,128)} %parent_last.1), channel_id=1, source_target_pairs={{0,8},{8,0},{16,24},{24,16},{1,9},{9,1},{17,25},{25,17},{2,10},{10... | collective-permute-start | bytes 4915208 | tf_op jit(solution)/shard_map/ppermute | solution.py:314
  192.4 39.3 %collective-permute-start.12 = (f32[640,640]{1,0:T(8,128)S(1)}, f32[640,640]{1,0:T(8,128)S(1)}, u32[]{:S(2)}, u32[]{:S(2)}) collective-permute-start(f32[640,640]{1,0:T(8,128)S(1)} %broadcast_select_fusion), channel_id=1, source_target_pairs={{0,1},{1,0},{2,3},{3,2},{4,5},{5,4},{6,7},{7,6},{8,9},{9,8},{10,11... | collective-permute-start | bytes 4915208 | tf_op jit(solution)/shard_map/ppermute | solution.py:314
  (1 other events, 0.7 us)
